TPU v7x, 32 devices: a whole 2x2x4 slice. The times are simulated.
32 devices in a mesh: dp: 16 (over z, x, core), tensor: 2 (over y).
Axes of the slice: x: 2, y: 2, z: 4, core: 2. Of those that a mesh axis runs over, the one named last changes fastest.
Arguments:
- inputs: bfloat16 [16, 2048, 512], P('dp', 'tensor'), may hold values from -6 to 6
- lengths: int32 [16], P('dp'), may hold values from 512 to 2048, as said below
- norm1_gain: float32 [512], replicated, may hold values from 0.25 to 1.75
- norm1_bias: float32 [512], replicated, may hold values from -4 to 4
- query_key_value_weight: bfloat16 [3, 512, 512], P(None, None, 'tensor'), may hold values from -0.25 to 0.25
- content_bias: float32 [8, 64], P('tensor'), may hold values from -6 to 6
- position_bias: float32 [8, 64], P('tensor'), may hold values from -6 to 6
- pos_weight: bfloat16 [512, 512], P(None, 'tensor'), may hold values from -0.25 to 0.25
- output_weight: bfloat16 [512, 512], P('tensor'), may hold values from -3 to 3
- out_bias: float32 [512], replicated, may hold values from -4 to 4
- norm2_gain: float32 [512], replicated, may hold values from 0.25 to 1.75
- norm2_bias: float32 [512], replicated, may hold values from -4 to 4
- up_projection_weight: bfloat16 [512, 2048], P(None, 'tensor'), may hold values from -0.25 to 0.25
- up_bias: float32 [2048], P('tensor'), may hold values from -4 to 4
- down_projection_weight: bfloat16 [2048, 512], P('tensor'), may hold values from -0.125 to 0.125
- down_bias: float32 [512], replicated, may hold values from -4 to 4
- cotangent: bfloat16 [16, 2048, 512], P('dp', 'tensor'), may hold values from -6 to 6
Outputs:
- output: bfloat16 [16, 2048, 512], P('dp', 'tensor')
- input_grad: float32 [16, 2048, 512], P('dp', 'tensor')
- norm1_gain_grad: float32 [512], replicated
- norm1_bias_grad: float32 [512], replicated
- qkv_weight_grad: float32 [3, 512, 512], P(None, None, 'tensor')
- content_bias_grad: float32 [8, 64], P('tensor')
- position_bias_grad: float32 [8, 64], P('tensor')
- pos_weight_grad: float32 [512, 512], P(None, 'tensor')
- out_weight_grad: float32 [512, 512], P('tensor')
- out_bias_grad: float32 [512], replicated
- norm2_gain_grad: float32 [512], replicated
- norm2_bias_grad: float32 [512], replicated
- up_projection_gradient: float32 [512, 2048], P(None, 'tensor')
- up_bias_grad: float32 [2048], P('tensor')
- down_weight_grad: float32 [2048, 512], P('tensor')
- down_bias_grad: float32 [512], replicated
Inputs may be any that keep to these rules, and one draw needn't show every extreme that they name: `lengths`: the valid tokens of a sequence are its first positions, the rest is padding. Every draw holds a sequence of 2048 and one of 512 tokens.
All inputs are finite; a program needn't handle non-finite values.
Results may differ from a plain program's by a relative error of at most 0.024.
Values may be sent and summed in bfloat16 or wider, within the bound.
No kernel may reach another device: no remote copies, remote signals or barrier semaphores. Data moves between devices by JAX's collectives and lax.ppermute only.
A program may use at most 192 MiB of HBM per device.

v0:
```python
import jax
import jax.numpy as jnp
from jax import lax
from jax.sharding import PartitionSpec as P

BLOCK = 512


epsilon = 1e-05
score_scale = 0.125
masked_score = -1e30


def gelu_exact(values):
    return jax.nn.gelu(values, approximate=False)


def norm_rows(values, norm_gain, norm_bias):
    centre = values - jnp.mean(values, axis=-1, keepdims=True)
    inverse = lax.rsqrt(jnp.mean(centre * centre, axis=-1, keepdims=True) + epsilon)
    normal = centre * inverse
    return (normal * norm_gain + norm_bias, normal, inverse)


def norm_back(upstream, normal, inverse, norm_gain):
    scaled = upstream * norm_gain
    centred = scaled - jnp.mean(scaled, axis=-1, keepdims=True)
    centred = centred - normal * jnp.mean(scaled * normal, axis=-1, keepdims=True)
    return (
        inverse * centred,
        jnp.sum(upstream * normal, axis=(0, 1)),
        jnp.sum(upstream, axis=(0, 1)),
    )


def sin_rows(row_count, model_width, seq_len):
    distance = (seq_len - 1 - jnp.arange(row_count, dtype=jnp.int32)).astype(jnp.float32)
    frequency = jnp.power(
        10000.0, -jnp.arange(0, model_width, 2, dtype=jnp.int32).astype(jnp.float32) / model_width
    )
    angles = distance[:, None] * frequency[None, :]
    return jnp.concatenate([jnp.sin(angles), jnp.cos(angles)], axis=1)


def shift_rows(wide_scores, key_count):
    head_count, row_count, column_count = wide_scores.shape
    flattened = wide_scores.reshape(head_count, row_count * column_count)
    trimmed = lax.slice_in_dim(
        flattened, row_count - 1, row_count - 1 + row_count * (column_count - 1), axis=1
    )
    return trimmed.reshape(head_count, row_count, column_count - 1)[:, :, :key_count]


def unshift_rows(narrow, column_count):
    head_count, row_count, key_count = narrow.shape
    padded = jnp.pad(narrow, ((0, 0), (0, 0), (0, column_count - 1 - key_count)))
    flattened = padded.reshape(head_count, row_count * (column_count - 1))
    flattened = jnp.pad(flattened, ((0, 0), (row_count - 1, 1)))
    return flattened.reshape(head_count, row_count, column_count)


def block_scores(query_part, offset_part, key_rows, position, block_index, key_block):
    seq_len = key_rows.shape[0]
    key_part = lax.dynamic_slice_in_dim(key_rows, key_block * BLOCK, BLOCK, 0)
    window = lax.dynamic_slice_in_dim(
        position, seq_len - (block_index - key_block + 1) * BLOCK, 2 * BLOCK, 0
    )
    content = jnp.einsum("rhe,che->hrc", query_part, key_part, preferred_element_type=jnp.float32)
    wide_scores = jnp.einsum(
        "rhe,khe->hrk", offset_part, window, preferred_element_type=jnp.float32
    )
    raw_scores = (content + shift_rows(wide_scores, BLOCK)) * score_scale
    row_pos = block_index * BLOCK + jnp.arange(BLOCK, dtype=jnp.int32)
    col_pos = key_block * BLOCK + jnp.arange(BLOCK, dtype=jnp.int32)
    allowed = row_pos[:, None] >= col_pos[None, :]
    return (jnp.where(allowed[None], raw_scores, masked_score), key_part, window)


def attend_sequence(query_content, query_offset, key_rows, value_rows, block_limit, position):
    seq_len, head_count, head_width = key_rows.shape
    block_count = seq_len // BLOCK

    def one_block(block_index):
        query_part = lax.dynamic_slice_in_dim(query_content, block_index * BLOCK, BLOCK, 0)
        offset_part = lax.dynamic_slice_in_dim(query_offset, block_index * BLOCK, BLOCK, 0)
        upper_bound = jnp.where(block_index < block_limit, block_index + 1, 0)

        def first_pass(key_block, state_carry):
            running_max, running_sum = state_carry
            scores = block_scores(
                query_part, offset_part, key_rows, position, block_index, key_block
            )[0]
            new_max = jnp.maximum(running_max, jnp.max(scores, axis=-1))
            running_sum = running_sum * jnp.exp(running_max - new_max) + jnp.sum(
                jnp.exp(scores - new_max[:, :, None]), axis=-1
            )
            return (new_max, running_sum)

        initial = (
            jnp.full((head_count, BLOCK), masked_score, jnp.float32),
            jnp.zeros((head_count, BLOCK), jnp.float32),
        )
        running_max, running_sum = lax.fori_loop(0, upper_bound, first_pass, initial)
        log_total = jnp.where(
            running_sum > 0,
            running_max + jnp.log(jnp.where(running_sum > 0, running_sum, 1.0)),
            0.0,
        )

        def second_pass(key_block, state_carry):
            out_low, out_remainder = state_carry
            scores = block_scores(
                query_part, offset_part, key_rows, position, block_index, key_block
            )[0]
            value_part = lax.dynamic_slice_in_dim(value_rows, key_block * BLOCK, BLOCK, 0)
            weights = jnp.exp(scores - log_total[:, :, None])
            rounded = weights.astype(jnp.bfloat16)
            remainder = (weights - rounded.astype(jnp.float32)).astype(jnp.bfloat16)
            out_low = out_low + jnp.einsum(
                "hrc,che->rhe", rounded, value_part, preferred_element_type=jnp.float32
            )
            out_remainder = out_remainder + jnp.einsum(
                "hrc,che->rhe", remainder, value_part, preferred_element_type=jnp.float32
            )
            return (out_low, out_remainder)

        zero_block = jnp.zeros((BLOCK, head_count, head_width), jnp.float32)
        out_low, out_remainder = lax.fori_loop(
            0, upper_bound, second_pass, (zero_block, zero_block)
        )
        return (out_low, out_low + out_remainder, log_total)

    out_low, out_exact, log_total = lax.map(one_block, jnp.arange(block_count, dtype=jnp.int32))
    return (
        out_low.reshape(seq_len, head_count, head_width),
        out_exact.reshape(seq_len, head_count, head_width),
        log_total,
    )


def attend_back(
    query_content,
    query_offset,
    key_rows,
    value_rows,
    out_grad,
    out_exact,
    log_total,
    block_limit,
    position,
):
    seq_len, head_count, head_width = key_rows.shape
    block_count = seq_len // BLOCK

    def one_block(state_carry, block_item):
        key_grad, value_grad, position_grad = state_carry
        block_index, block_total = block_item
        query_part = lax.dynamic_slice_in_dim(query_content, block_index * BLOCK, BLOCK, 0)
        offset_part = lax.dynamic_slice_in_dim(query_offset, block_index * BLOCK, BLOCK, 0)
        grad_part = lax.dynamic_slice_in_dim(out_grad, block_index * BLOCK, BLOCK, 0)
        exact_part = lax.dynamic_slice_in_dim(out_exact, block_index * BLOCK, BLOCK, 0)
        row_delta = jnp.einsum("rhe,rhe->hr", grad_part.astype(jnp.float32), exact_part)
        upper_bound = jnp.where(block_index < block_limit, block_index + 1, 0)

        def inner_step(key_block, inner_carry):
            content_grad, offset_grad, key_grad, value_grad, position_grad = inner_carry
            scores, key_part, window = block_scores(
                query_part, offset_part, key_rows, position, block_index, key_block
            )
            key_start = key_block * BLOCK
            value_part = lax.dynamic_slice_in_dim(value_rows, key_start, BLOCK, 0)
            weights = jnp.exp(scores - block_total[:, :, None])
            weight_grad = jnp.einsum(
                "rhe,che->hrc", grad_part, value_part, preferred_element_type=jnp.float32
            )
            score_grad = (weights * (weight_grad - row_delta[:, :, None]) * score_scale).astype(
                jnp.bfloat16
            )
            value_add = jnp.einsum(
                "hrc,rhe->che",
                weights.astype(jnp.bfloat16),
                grad_part,
                preferred_element_type=jnp.float32,
            )
            key_add = jnp.einsum(
                "hrc,rhe->che", score_grad, query_part, preferred_element_type=jnp.float32
            )
            content_grad = content_grad + jnp.einsum(
                "hrc,che->rhe", score_grad, key_part, preferred_element_type=jnp.float32
            )
            wide_grad = unshift_rows(score_grad, 2 * BLOCK)
            offset_grad = offset_grad + jnp.einsum(
                "hrk,khe->rhe", wide_grad, window, preferred_element_type=jnp.float32
            )
            window_add = jnp.einsum(
                "hrk,rhe->khe", wide_grad, offset_part, preferred_element_type=jnp.float32
            )
            key_grad = lax.dynamic_update_slice_in_dim(
                key_grad,
                lax.dynamic_slice_in_dim(key_grad, key_start, BLOCK, 0) + key_add,
                key_start,
                0,
            )
            value_grad = lax.dynamic_update_slice_in_dim(
                value_grad,
                lax.dynamic_slice_in_dim(value_grad, key_start, BLOCK, 0) + value_add,
                key_start,
                0,
            )
            window_start = seq_len - (block_index - key_block + 1) * BLOCK
            position_grad = lax.dynamic_update_slice_in_dim(
                position_grad,
                lax.dynamic_slice_in_dim(position_grad, window_start, 2 * BLOCK, 0) + window_add,
                window_start,
                0,
            )
            return (content_grad, offset_grad, key_grad, value_grad, position_grad)

        zero_block = jnp.zeros((BLOCK, head_count, head_width), jnp.float32)
        content_grad, offset_grad, key_grad, value_grad, position_grad = lax.fori_loop(
            0,
            upper_bound,
            inner_step,
            (zero_block, zero_block, key_grad, value_grad, position_grad),
        )
        return ((key_grad, value_grad, position_grad), (content_grad, offset_grad))

    initial = (
        jnp.zeros((seq_len, head_count, head_width), jnp.float32),
        jnp.zeros((seq_len, head_count, head_width), jnp.float32),
        jnp.zeros((position.shape[0], head_count, head_width), jnp.float32),
    )
    (key_grad, value_grad, position_grad), (content_grad, offset_grad) = lax.scan(
        one_block, initial, (jnp.arange(block_count, dtype=jnp.int32), log_total)
    )
    return (
        content_grad.reshape(seq_len, head_count, head_width),
        offset_grad.reshape(seq_len, head_count, head_width),
        key_grad,
        value_grad,
        position_grad,
    )


def local(
    inputs,
    lengths,
    norm1_gain,
    norm1_bias,
    query_key_value_weight,
    content_bias,
    position_bias,
    pos_weight,
    output_weight,
    out_bias,
    norm2_gain,
    norm2_bias,
    up_projection_weight,
    up_bias,
    down_projection_weight,
    down_bias,
    cotangent,
):
    tensor_count = lax.axis_size("tensor")
    seq_count, shard_rows, model_width = inputs.shape
    seq_len = shard_rows * tensor_count
    head_count, head_width = content_bias.shape
    local_width = head_count * head_width
    shaped = (seq_count, seq_len, head_count, head_width)
    flat_shape = (seq_count, seq_len, local_width)
    offset = lax.axis_index("tensor") * shard_rows
    shard_valid = (
        (offset + jnp.arange(shard_rows, dtype=jnp.int32))[None, :] < lengths[:, None]
    ).astype(jnp.float32)[:, :, None]
    full_valid = (jnp.arange(seq_len, dtype=jnp.int32)[None, :] < lengths[:, None]).astype(
        jnp.bfloat16
    )[:, :, None]
    block_limit = jnp.full((seq_count,), seq_len // BLOCK, jnp.int32)
    sin_table = sin_rows(seq_len + BLOCK, model_width, seq_len).astype(jnp.bfloat16)
    position = jnp.dot(sin_table, pos_weight, preferred_element_type=jnp.float32).astype(
        jnp.bfloat16
    )
    position_heads = position.reshape(-1, head_count, head_width)

    def front(source):
        normed1, unit1, inverse1 = norm_rows(source, norm1_gain, norm1_bias)
        first_rows = lax.all_gather(normed1.astype(jnp.bfloat16), "tensor", axis=1, tiled=True)
        projected = jnp.einsum(
            "tpr,nrk->ntpk", first_rows, query_key_value_weight, preferred_element_type=jnp.float32
        )
        query_content = (
            (projected[0] + content_bias.reshape(-1)).astype(jnp.bfloat16).reshape(shaped)
        )
        query_offset = (
            (projected[0] + position_bias.reshape(-1)).astype(jnp.bfloat16).reshape(shaped)
        )
        key_rows = projected[1].astype(jnp.bfloat16).reshape(shaped)
        value_rows = projected[2].astype(jnp.bfloat16).reshape(shaped)
        out_low, out_exact, log_total = lax.map(
            lambda seq_item: attend_sequence(
                seq_item[0], seq_item[1], seq_item[2], seq_item[3], seq_item[4], position_heads
            ),
            (query_content, query_offset, key_rows, value_rows, block_limit),
        )
        attention_result = out_low.reshape(flat_shape).astype(jnp.bfloat16)
        head_terms = jnp.einsum(
            "apb,bu->apu", attention_result, output_weight, preferred_element_type=jnp.float32
        )
        middle = source + (
            lax.psum_scatter(head_terms, "tensor", scatter_dimension=1, tiled=True) + out_bias
        )
        normed2, unit2, inverse2 = norm_rows(middle, norm2_gain, norm2_bias)
        second_rows = lax.all_gather(normed2.astype(jnp.bfloat16), "tensor", axis=1, tiled=True)
        hidden_pre = (
            jnp.einsum(
                "yoz,zk->yok", second_rows, up_projection_weight, preferred_element_type=jnp.float32
            )
            + up_bias
        )
        return (
            unit1,
            inverse1,
            first_rows,
            query_content,
            query_offset,
            key_rows,
            value_rows,
            out_exact,
            log_total,
            attention_result,
            middle,
            unit2,
            inverse2,
            second_rows,
            hidden_pre,
        )

    source = inputs.astype(jnp.float32)
    kept = front(source)
    active_mask, gelu_pull = jax.vjp(gelu_exact, kept[14])
    down_terms = jnp.einsum(
        "ebv,vh->ebh",
        active_mask.astype(jnp.bfloat16),
        down_projection_weight,
        preferred_element_type=jnp.float32,
    )
    ffn_out = (
        lax.psum_scatter(
            down_terms.astype(jnp.bfloat16), "tensor", scatter_dimension=1, tiled=True
        ).astype(jnp.float32)
        + down_bias
    )
    output = (shard_valid * (kept[10] + ffn_out)).astype(jnp.bfloat16)
    barrier_pair = lax.optimization_barrier((source, output))
    kept = front(barrier_pair[0])
    active_mask, gelu_pull = jax.vjp(gelu_exact, kept[14])
    (
        unit1,
        inverse1,
        first_rows,
        query_content,
        query_offset,
        key_rows,
        value_rows,
        out_exact,
        log_total,
        attention_result,
        middle,
        unit2,
        inverse2,
        second_rows,
        hidden_pre,
    ) = kept
    grad_rows = cotangent.astype(jnp.float32) * shard_valid
    complete_gradient = lax.all_gather(cotangent, "tensor", axis=1, tiled=True) * full_valid
    down_weight_grad = jnp.einsum(
        "igt,igc->tc",
        active_mask.astype(jnp.bfloat16),
        complete_gradient,
        preferred_element_type=jnp.float32,
    )
    hidden_grad = jnp.einsum(
        "bha,za->bhz", complete_gradient, down_projection_weight, preferred_element_type=jnp.float32
    )
    preceding_gradient = gelu_pull(hidden_grad)[0].astype(jnp.bfloat16)
    up_projection_gradient = jnp.einsum(
        "vji,vjo->io", second_rows, preceding_gradient, preferred_element_type=jnp.float32
    )
    up_bias_grad = jnp.sum(preceding_gradient.astype(jnp.float32), axis=(0, 1))
    second_rows_gradient = jnp.einsum(
        "hck,vk->hcv", preceding_gradient, up_projection_weight, preferred_element_type=jnp.float32
    )
    middle_part, gain2_grad, bias2_grad = norm_back(
        lax.psum_scatter(second_rows_gradient, "tensor", scatter_dimension=1, tiled=True),
        unit2,
        inverse2,
        norm2_gain,
    )
    middle_grad = grad_rows + middle_part
    branch_grad = middle_grad.astype(jnp.bfloat16)
    complete_branch = lax.all_gather(branch_grad, "tensor", axis=1, tiled=True)
    out_weight_grad = jnp.einsum(
        "eyn,eyb->nb", attention_result, complete_branch, preferred_element_type=jnp.float32
    )
    attended_grad = (
        jnp.einsum(
            "cop,np->con", complete_branch, output_weight, preferred_element_type=jnp.float32
        )
        .astype(jnp.bfloat16)
        .reshape(shaped)
    )
    content_grad, offset_grad, key_grad, value_grad, position_grad = lax.map(
        lambda seq_item: attend_back(
            seq_item[0],
            seq_item[1],
            seq_item[2],
            seq_item[3],
            seq_item[4],
            seq_item[5],
            seq_item[6],
            seq_item[7],
            position_heads,
        ),
        (
            query_content,
            query_offset,
            key_rows,
            value_rows,
            attended_grad,
            out_exact,
            log_total,
            block_limit,
        ),
    )
    query_grad = (content_grad + offset_grad).reshape(flat_shape)
    stacked_gradient = jnp.stack(
        [query_grad, key_grad.reshape(flat_shape), value_grad.reshape(flat_shape)]
    ).astype(jnp.bfloat16)
    qkv_weight_grad = jnp.einsum(
        "pir,epiq->erq", first_rows, stacked_gradient, preferred_element_type=jnp.float32
    )
    content_bias_grad = jnp.sum(content_grad, axis=(0, 1))
    position_bias_grad = jnp.sum(offset_grad, axis=(0, 1))
    position_rows = position_grad.reshape(seq_count, -1, local_width).astype(jnp.bfloat16)
    pos_weight_grad = jnp.einsum(
        "nd,snh->dh", sin_table, position_rows, preferred_element_type=jnp.float32
    )
    rows1_grad = jnp.einsum(
        "zjew,zkw->jek",
        stacked_gradient,
        query_key_value_weight,
        preferred_element_type=jnp.float32,
    )
    rows1_upstream = lax.psum_scatter(
        rows1_grad.astype(jnp.bfloat16), "tensor", scatter_dimension=1, tiled=True
    ).astype(jnp.float32)
    input_part, gain1_grad, bias1_grad = norm_back(rows1_upstream, unit1, inverse1, norm1_gain)
    input_grad = middle_grad + input_part
    weight_sums = (
        lax.psum(qkv_weight_grad.astype(jnp.bfloat16), "dp").astype(jnp.float32),
        lax.psum(content_bias_grad.astype(jnp.bfloat16), "dp").astype(jnp.float32),
        lax.psum(position_bias_grad.astype(jnp.bfloat16), "dp").astype(jnp.float32),
        lax.psum(pos_weight_grad.astype(jnp.bfloat16), "dp").astype(jnp.float32),
        lax.psum(out_weight_grad.astype(jnp.bfloat16), "dp").astype(jnp.float32),
        lax.psum(up_projection_gradient.astype(jnp.bfloat16), "dp").astype(jnp.float32),
        lax.psum(up_bias_grad.astype(jnp.bfloat16), "dp").astype(jnp.float32),
        lax.psum(down_weight_grad.astype(jnp.bfloat16), "dp").astype(jnp.float32),
    )
    norm_sums = lax.psum(
        jnp.stack(
            [
                gain1_grad,
                bias1_grad,
                jnp.sum(branch_grad.astype(jnp.float32), axis=(0, 1)),
                gain2_grad,
                bias2_grad,
                jnp.sum(grad_rows, axis=(0, 1)),
            ]
        ),
        ("dp", "tensor"),
    )
    return (
        output,
        input_grad,
        norm_sums[0],
        norm_sums[1],
        weight_sums[0],
        weight_sums[1],
        weight_sums[2],
        weight_sums[3],
        weight_sums[4],
        norm_sums[2],
        norm_sums[3],
        norm_sums[4],
        weight_sums[5],
        weight_sums[6],
        weight_sums[7],
        norm_sums[5],
    )


def solution(mesh):
    return jax.shard_map(
        local,
        mesh=mesh,
        in_specs=(
            P("dp", "tensor", None),
            P("dp"),
            P(),
            P(),
            P(None, None, "tensor"),
            P("tensor", None),
            P("tensor", None),
            P(None, "tensor"),
            P("tensor", None),
            P(),
            P(),
            P(),
            P(None, "tensor"),
            P("tensor"),
            P("tensor", None),
            P(),
            P("dp", "tensor", None),
        ),
        out_specs=(
            P("dp", "tensor", None),
            P("dp", "tensor", None),
            P(),
            P(),
            P(None, None, "tensor"),
            P("tensor", None),
            P("tensor", None),
            P(None, "tensor"),
            P("tensor", None),
            P(),
            P(),
            P(),
            P(None, "tensor"),
            P("tensor"),
            P("tensor", None),
            P(),
        ),
        check_vma=False,
    )
```

profile of v0, /device:TPU:0, one launch (start us, length us, event | category | flops | bytes accessed | tf_op | source)
XLA Modules:
  0.0 4777.0 jit_solution(15370454987708482289)
XLA Ops:
  62.8 1371.2 %while.221 = (s32[]{:T(128)}, bf16[4,512,4,64]{1,3,2,0:T(8,128)(2,1)}, s32[4]{0:T(128)}, bf16[2048,4,64]{0,2,1:T(8,128)(2,1)}, bf16[2048,4,64]{0,2,1:T(8,128)(2,...) while((s32[]{:T(128)}, ...), condition=%wide.region_9.10_spmd, body=%wide.region_2.9_spmd.sunk | while | flops 951728128 | bytes 195667600 | solution.py:133
  71.6 78.1 %while.227 = (s32[]{:T(128)}, f32[4,512]{1,0:T(4,128)S(1)}, f32[4,512]{1,0:T(4,128)S(1)}, s32[]{:T(128)}, s32[]{:T(128)}, /*index=5*/bf16[2048,4,64]{0,2,1:T(8,1...) while((s32[]{:T(128)}, f32[4,512]{1,0:T(4,128)S(1)}, ...), condition=%wide.region_6.6_spmd, body=%wide.region_3.5_spmd.sunk | while | flops 409211904 | bytes 106774816 | solution.py:103
  151.6 57.7 %while.228 = (s32[]{:T(128)}, f32[512,4,64]{0,2,1:T(8,128)}, s32[]{:T(128)}, bf16[2048,4,64]{0,2,1:T(8,128)(2,1)}, s32[]{:T(128)}, /*index=5*/bf16[2048,4,64]{2,...) while((s32[]{:T(128)}, f32[512,4,64]{0,2,1:T(8,128)}, ...), condition=%wide.region_8.8_spmd, body=%wide.region_7.7_spmd.sunk | while | flops 542508032 | bytes 83607848 | solution.py:128
  232.4 143.2 %while.227 = (s32[]{:T(128)}, f32[4,512]{1,0:T(4,128)S(1)}, f32[4,512]{1,0:T(4,128)S(1)}, s32[]{:T(128)}, s32[]{:T(128)}, /*index=5*/bf16[2048,4,64]{0,2,1:T(8,1...) while((s32[]{:T(128)}, f32[4,512]{1,0:T(4,128)S(1)}, ...), condition=%wide.region_6.6_spmd, body=%wide.region_3.5_spmd.sunk | while | flops 409211904 | bytes 106774816 | solution.py:103
  377.6 115.4 %while.228 = (s32[]{:T(128)}, f32[512,4,64]{0,2,1:T(8,128)}, s32[]{:T(128)}, bf16[2048,4,64]{0,2,1:T(8,128)(2,1)}, s32[]{:T(128)}, /*index=5*/bf16[2048,4,64]{2,...) while((s32[]{:T(128)}, f32[512,4,64]{0,2,1:T(8,128)}, ...), condition=%wide.region_8.8_spmd, body=%wide.region_7.7_spmd.sunk | while | flops 542508032 | bytes 83607848 | solution.py:128
  516.1 208.5 %while.227 = (s32[]{:T(128)}, f32[4,512]{1,0:T(4,128)S(1)}, f32[4,512]{1,0:T(4,128)S(1)}, s32[]{:T(128)}, s32[]{:T(128)}, /*index=5*/bf16[2048,4,64]{0,2,1:T(8,1...) while((s32[]{:T(128)}, f32[4,512]{1,0:T(4,128)S(1)}, ...), condition=%wide.region_6.6_spmd, body=%wide.region_3.5_spmd.sunk | while | flops 409211904 | bytes 106774816 | solution.py:103
  726.5 173.1 %while.228 = (s32[]{:T(128)}, f32[512,4,64]{0,2,1:T(8,128)}, s32[]{:T(128)}, bf16[2048,4,64]{0,2,1:T(8,128)(2,1)}, s32[]{:T(128)}, /*index=5*/bf16[2048,4,64]{2,...) while((s32[]{:T(128)}, f32[512,4,64]{0,2,1:T(8,128)}, ...), condition=%wide.region_8.8_spmd, body=%wide.region_7.7_spmd.sunk | while | flops 542508032 | bytes 83607848 | solution.py:128
  922.7 273.7 %while.227 = (s32[]{:T(128)}, f32[4,512]{1,0:T(4,128)S(1)}, f32[4,512]{1,0:T(4,128)S(1)}, s32[]{:T(128)}, s32[]{:T(128)}, /*index=5*/bf16[2048,4,64]{0,2,1:T(8,1...) while((s32[]{:T(128)}, f32[4,512]{1,0:T(4,128)S(1)}, ...), condition=%wide.region_6.6_spmd, body=%wide.region_3.5_spmd.sunk | while | flops 409211904 | bytes 106774816 | solution.py:103
  1198.4 230.8 %while.228 = (s32[]{:T(128)}, f32[512,4,64]{0,2,1:T(8,128)}, s32[]{:T(128)}, bf16[2048,4,64]{0,2,1:T(8,128)(2,1)}, s32[]{:T(128)}, /*index=5*/bf16[2048,4,64]{2,...) while((s32[]{:T(128)}, f32[512,4,64]{0,2,1:T(8,128)}, ...), condition=%wide.region_8.8_spmd, body=%wide.region_7.7_spmd.sunk | while | flops 542508032 | bytes 83607848 | solution.py:128
  1439.3 54.4 %reduce-scatter.6.cloned.1.call-done = f32[1,1024,512]{2,1,0:T(8,128)} async-done(((f32[1,2048,512]{2,1,0:T(8,128)}), f32[1,1024,512]{2,1,0:T(8,128)}) %reduce-scatter.6.cloned.1.call-update) | async-done | bytes 2097168 | tf_op jit(solution)/shard_map/reduce_scatter | solution.py:310
  1498.2 33.2 all-gather.9.cloned.1.call-done
  1597.8 33.2 all-gather.11.cloned.1.call-done
  1640.5 1453.7 %while.224 = (s32[]{:T(128)}, bf16[4,512,4,64]{1,3,2,0:T(8,128)(2,1)}, f32[4,512,4,64]{1,3,2,0:T(8,128)}, f32[4,4,512]{2,1,0:T(4,128)}, s32[4]{0:T(128)}, /*inde...) while((s32[]{:T(128)}, ...), condition=%wide.region_23.24_spmd, body=%wide.region_16.23_spmd.sunk | while | flops 1090402304 | bytes 232900880 | solution.py:133
  1645.1 65.2 %while.229 = (s32[]{:T(128)}, f32[4,512]{1,0:T(4,128)S(1)}, f32[4,512]{1,0:T(4,128)S(1)}, s32[]{:T(128)}, s32[]{:T(128)}, /*index=5*/bf16[2048,4,64]{0,2,1:T(8,1...) while((s32[]{:T(128)}, f32[4,512]{1,0:T(4,128)S(1)}, ...), condition=%wide.region_20.20_spmd, body=%wide.region_17.19_spmd.sunk | while | flops 409211904 | bytes 106774816 | solution.py:103
  1711.9 80.3 %while.230 = (s32[]{:T(128)}, f32[512,4,64]{0,2,1:T(8,128)S(1)}, f32[512,4,64]{0,2,1:T(8,128)}, s32[]{:T(128)}, bf16[2048,4,64]{0,2,1:T(8,128)(2,1)}, /*index=5*...) while((s32[]{:T(128)}, f32[512,4,64]{0,2,1:T(8,128)S(1)}, ...), condition=%wide.region_22.22_spmd, body=%wide.region_21.21_spmd.sunk | while | flops 681051136 | bytes 121880968 | solution.py:128
  1809.4 130.5 %while.229 = (s32[]{:T(128)}, f32[4,512]{1,0:T(4,128)S(1)}, f32[4,512]{1,0:T(4,128)S(1)}, s32[]{:T(128)}, s32[]{:T(128)}, /*index=5*/bf16[2048,4,64]{0,2,1:T(8,1...) while((s32[]{:T(128)}, f32[4,512]{1,0:T(4,128)S(1)}, ...), condition=%wide.region_20.20_spmd, body=%wide.region_17.19_spmd.sunk | while | flops 409211904 | bytes 106774816 | solution.py:103
  1941.4 147.3 %while.230 = (s32[]{:T(128)}, f32[512,4,64]{0,2,1:T(8,128)S(1)}, f32[512,4,64]{0,2,1:T(8,128)}, s32[]{:T(128)}, bf16[2048,4,64]{0,2,1:T(8,128)(2,1)}, /*index=5*...) while((s32[]{:T(128)}, f32[512,4,64]{0,2,1:T(8,128)S(1)}, ...), condition=%wide.region_22.22_spmd, body=%wide.region_21.21_spmd.sunk | while | flops 681051136 | bytes 121880968 | solution.py:128
  2106.0 195.7 %while.229 = (s32[]{:T(128)}, f32[4,512]{1,0:T(4,128)S(1)}, f32[4,512]{1,0:T(4,128)S(1)}, s32[]{:T(128)}, s32[]{:T(128)}, /*index=5*/bf16[2048,4,64]{0,2,1:T(8,1...) while((s32[]{:T(128)}, f32[4,512]{1,0:T(4,128)S(1)}, ...), condition=%wide.region_20.20_spmd, body=%wide.region_17.19_spmd.sunk | while | flops 409211904 | bytes 106774816 | solution.py:103
  2303.2 214.3 %while.230 = (s32[]{:T(128)}, f32[512,4,64]{0,2,1:T(8,128)S(1)}, f32[512,4,64]{0,2,1:T(8,128)}, s32[]{:T(128)}, bf16[2048,4,64]{0,2,1:T(8,128)(2,1)}, /*index=5*...) while((s32[]{:T(128)}, f32[512,4,64]{0,2,1:T(8,128)S(1)}, ...), condition=%wide.region_22.22_spmd, body=%wide.region_21.21_spmd.sunk | while | flops 681051136 | bytes 121880968 | solution.py:128
  2534.7 260.9 %while.229 = (s32[]{:T(128)}, f32[4,512]{1,0:T(4,128)S(1)}, f32[4,512]{1,0:T(4,128)S(1)}, s32[]{:T(128)}, s32[]{:T(128)}, /*index=5*/bf16[2048,4,64]{0,2,1:T(8,1...) while((s32[]{:T(128)}, f32[4,512]{1,0:T(4,128)S(1)}, ...), condition=%wide.region_20.20_spmd, body=%wide.region_17.19_spmd.sunk | while | flops 409211904 | bytes 106774816 | solution.py:103
  2797.2 281.3 %while.230 = (s32[]{:T(128)}, f32[512,4,64]{0,2,1:T(8,128)S(1)}, f32[512,4,64]{0,2,1:T(8,128)}, s32[]{:T(128)}, bf16[2048,4,64]{0,2,1:T(8,128)(2,1)}, /*index=5*...) while((s32[]{:T(128)}, f32[512,4,64]{0,2,1:T(8,128)S(1)}, ...), condition=%wide.region_22.22_spmd, body=%wide.region_21.21_spmd.sunk | while | flops 681051136 | bytes 121880968 | solution.py:128
  3100.3 54.4 %reduce-scatter.10.cloned.1.call-done = f32[1,1024,512]{2,1,0:T(8,128)} async-done(((f32[1,2048,512]{2,1,0:T(8,128)}), f32[1,1024,512]{2,1,0:T(8,128)}) %reduce-scatter.10.cloned.1.call-update) | async-done | bytes 2097168 | tf_op jit(solution)/shard_map/reduce_scatter | solution.py:310
  3160.7 32.5 all-gather.13.cloned.1.call-done
  3244.8 54.4 %reduce-scatter.12.cloned.1.call-done = f32[1,1024,512]{2,1,0:T(8,128)} async-done(((f32[1,2048,512]{2,1,0:T(8,128)}), f32[1,1024,512]{2,1,0:T(8,128)}) %reduce-scatter.12.cloned.1.call-update) | async-done | bytes 2097168 | tf_op jit(solution)/shard_map/reduce_scatter | solution.py:394
  3351.5 1205.0 %while.226 = (s32[]{:T(128)}, f32[2048,4,64]{0,2,1:T(8,128)}, f32[2048,4,64]{0,2,1:T(8,128)}, f32[2560,4,64]{0,2,1:T(8,128)}, f32[4,512,4,64]{1,3,2,0:T(8,128)},...) while((s32[]{:T(128)}, f32[2048,4,64]{0,2,1:T(8,128)}, ...), condition=%wide.region_33.34_spmd, body=%wide.region_30.33_spmd.sunk | while | flops 1487272960 | bytes 254551888 | solution.py:233
  3387.0 110.9 %while.231 = (s32[]{:T(128)}, f32[512,4,64]{0,2,1:T(8,128)}, f32[512,4,64]{0,2,1:T(8,128)}, f32[2048,4,64]{0,2,1:T(8,128)}, f32[2048,4,64]{0,2,1:T(8,128)}, /*in...) while((s32[]{:T(128)}, f32[512,4,64]{0,2,1:T(8,128)}, ...), condition=%wide.region_32.32_spmd, body=%wide.region_31.31_spmd.sunk | while | flops 1486881792 | bytes 247169840 | solution.py:220
  3514.7 221.8 %while.231 = (s32[]{:T(128)}, f32[512,4,64]{0,2,1:T(8,128)}, f32[512,4,64]{0,2,1:T(8,128)}, f32[2048,4,64]{0,2,1:T(8,128)}, f32[2048,4,64]{0,2,1:T(8,128)}, /*in...) while((s32[]{:T(128)}, f32[512,4,64]{0,2,1:T(8,128)}, ...), condition=%wide.region_32.32_spmd, body=%wide.region_31.31_spmd.sunk | while | flops 1486881792 | bytes 247169840 | solution.py:220
  3753.3 332.8 %while.231 = (s32[]{:T(128)}, f32[512,4,64]{0,2,1:T(8,128)}, f32[512,4,64]{0,2,1:T(8,128)}, f32[2048,4,64]{0,2,1:T(8,128)}, f32[2048,4,64]{0,2,1:T(8,128)}, /*in...) while((s32[]{:T(128)}, f32[512,4,64]{0,2,1:T(8,128)}, ...), condition=%wide.region_32.32_spmd, body=%wide.region_31.31_spmd.sunk | while | flops 1486881792 | bytes 247169840 | solution.py:220
  4102.9 443.7 %while.231 = (s32[]{:T(128)}, f32[512,4,64]{0,2,1:T(8,128)}, f32[512,4,64]{0,2,1:T(8,128)}, f32[2048,4,64]{0,2,1:T(8,128)}, f32[2048,4,64]{0,2,1:T(8,128)}, /*in...) while((s32[]{:T(128)}, f32[512,4,64]{0,2,1:T(8,128)}, ...), condition=%wide.region_32.32_spmd, body=%wide.region_31.31_spmd.sunk | while | flops 1486881792 | bytes 247169840 | solution.py:220
  4589.1 33.9 all-reduce.2
  4624.7 66.4 %all-reduce.6.cloned.1.call-done = (bf16[3,512,256]{1,2,0:T(8,128)(2,1)}, bf16[512,256]{1,0:T(8,128)(2,1)}, bf16[256,512]{1,0:T(8,128)(2,1)}, bf16[512,1024]{1,0:T(8,128)(2,1)}, bf16[1024,512]{1,0:T(8,128)(2,1)}) async-done(((bf16[3,512,256]{1,2,0:T(8,128)(2,1)}, bf16[512,256]{1,0:T(8,128)(2,1)}, bf16[256,512]{1,0:T(8,128)(2,1)}, bf16[512,1024]{1,0:T(8,128)(2,1)}, bf16[1024,512]{1,0:T(8,128)(2,1)}), ...) | async-done | bytes 3407888 | tf_op jit(solution)/shard_map/psum | solution.py:460
  4726.7 39.4 psum.63
  (1391 shorter events, 4076.9 us)
Async XLA Ops:
  7.2 1524.2 %copy-start = (bf16[512,1024]{1,0:T(8,128)(2,1)S(1)}, bf16[512,1024]{1,0:T(8,128)(2,1)}, u32[]{:S(2)}) copy-start(bf16[512,1024]{1,0:T(8,128)(2,1)} %param.45) | copy-start | bytes 3145732
  7.2 42.0 all-gather.7.cloned.1.call-start
  13.2 1480.4 %reduce-scatter.6.cloned.1.call-start = ((), (), s32[]{:S(2)}) async-start(), calls=%async_computation.6 | async-start | bytes 6291456 | tf_op jit(solution)/shard_map/reduce_scatter | solution.py:310
  15.3 33.9 copy-start.28
  1436.5 57.2 %copy-start.20 = (bf16[1,1024,512]{2,1,0:T(8,128)(2,1)S(1)}, bf16[1,1024,512]{2,1,0:T(8,128)(2,1)}, u32[]{:S(2)}) copy-start(bf16[1,1024,512]{2,1,0:T(8,128)(2,1)} %param.33) | copy-start | bytes 3145732
  1436.5 57.2 %copy-start.51 = (f32[512]{0:T(512)S(1)}, f32[512]{0:T(512)}, u32[]{:S(2)}) copy-start(f32[512]{0:T(512)} %param.42) | copy-start | bytes 6148
  1439.2 57.3 %copy-start.55 = (f32[512]{0:T(512)S(1)}, f32[512]{0:T(512)}, u32[]{:S(2)}) copy-start(f32[512]{0:T(512)} %param.43) | copy-start | bytes 6148
  1439.2 57.3 %copy-start.63 = (f32[512]{0:T(512)S(1)}, f32[512]{0:T(512)}, u32[]{:S(2)}) copy-start(f32[512]{0:T(512)} %param.44) | copy-start | bytes 6148
  1439.2 92.2 %all-gather.9.cloned.1.call-start = ((), (), s32[]{:S(2)}) async-start(), calls=%async_computation.7 | async-start | bytes 3145728 | tf_op jit(solution)/shard_map/all_gather | solution.py:313
  1495.9 35.5 copy-start.47
  1498.1 88.7 %reduce-scatter.8.cloned.1.call-start = ((), (), s32[]{:S(2)}) async-start(), calls=%async_computation.8 | async-start | bytes 3145728 | tf_op jit(solution)/shard_map/reduce_scatter | solution.py:348
  1554.8 32.0 copy-start.70
  1554.8 76.2 %all-gather.11.cloned.1.call-start = ((), (), s32[]{:S(2)}) async-start(), calls=%async_computation.9 | async-start | bytes 3145728 | tf_op jit(solution)/shard_map/all_gather | solution.py:287
  1557.4 36.8 copy-start.53
  1557.4 37.4 copy-start.57
  1557.4 37.4 copy-start.67
  1590.2 40.8 copy-start.29
  1597.7 1557.0 %reduce-scatter.10.cloned.1.call-start = ((), (), s32[]{:S(2)}) async-start(), calls=%async_computation.10 | async-start | bytes 6291456 | tf_op jit(solution)/shard_map/reduce_scatter | solution.py:310
  3097.5 57.2 %copy-start.52 = (f32[512]{0:T(512)S(1)}, f32[512]{0:T(512)}, u32[]{:S(2)}) copy-start(f32[512]{0:T(512)} %param.42) | copy-start | bytes 6148
  3100.2 58.3 %copy-start.56 = (f32[512]{0:T(512)S(1)}, f32[512]{0:T(512)}, u32[]{:S(2)}) copy-start(f32[512]{0:T(512)} %param.43) | copy-start | bytes 6148
  3100.3 58.3 %copy-start.64 = (f32[512]{0:T(512)S(1)}, f32[512]{0:T(512)}, u32[]{:S(2)}) copy-start(f32[512]{0:T(512)} %param.44) | copy-start | bytes 6148
  3100.3 92.9 %all-gather.13.cloned.1.call-start = ((), (), s32[]{:S(2)}) async-start(), calls=%async_computation.11 | async-start | bytes 3145728 | tf_op jit(solution)/shard_map/all_gather | solution.py:313
  3157.2 36.0 copy-start.48
  3159.9 68.0 %all-gather.15.cloned.1.call-start = ((), (), s32[]{:S(2)}) async-start(), calls=%async_computation.12 | async-start | bytes 3145728 | tf_op jit(solution)/shard_map/all_gather | solution.py:375
  3160.7 138.6 %reduce-scatter.12.cloned.1.call-start = ((), (), s32[]{:S(2)}) async-start(), calls=%async_computation.13 | async-start | bytes 6291456 | tf_op jit(solution)/shard_map/reduce_scatter | solution.py:394
  3160.7 67.2 %copy-start.73 = (bf16[1024,512]{1,0:T(8,128)(2,1)S(1)}, bf16[1024,512]{1,0:T(8,128)(2,1)}, u32[]{:S(2)}) copy-start(bf16[1024,512]{1,0:T(8,128)(2,1)} %param.47) | copy-start | bytes 3145732
  3244.7 58.4 %copy-start.31 = (bf16[1,1024,512]{2,1,0:T(8,128)(2,1)S(1)}, bf16[1,1024,512]{2,1,0:T(8,128)(2,1)}, u32[]{:S(2)}) copy-start(bf16[1,1024,512]{2,1,0:T(8,128)(2,1)} %param.49) | copy-start | bytes 3145732
  3244.7 58.4 %copy-start.54 = (f32[1024]{0:T(1024)S(1)}, f32[1024]{0:T(1024)}, u32[]{:S(2)}) copy-start(f32[1024]{0:T(1024)} %copy-done.53) | copy-start | bytes 12292
  3244.8 94.8 %all-gather.17.cloned.1.call-start = ((), (), s32[]{:S(2)}) async-start(), calls=%async_computation.14 | async-start | bytes 3145728 | tf_op jit(solution)/shard_map/all_gather | solution.py:401
  3306.3 1384.9 %all-reduce.6.cloned.1.call-start = ((), (), s32[]{:S(2)}) async-start(), calls=%async_computation.16 | async-start | bytes 6815744 | tf_op jit(solution)/shard_map/psum | solution.py:460
  4584.2 140.0 %reduce-scatter.14.cloned.1.call-start = ((), (), s32[]{:S(2)}) async-start(), calls=%async_computation.15 | async-start | bytes 3145728 | tf_op jit(solution)/shard_map/reduce_scatter | solution.py:454
  4694.0 30.3 copy-start.58
  (209 other events, 1016.1 us)
Sparse Core Ops, SparseCore 0:
  13.3 35.8 all-gather.6
  1439.3 54.2 reduce-scatter.5
  1498.3 33.1 all-gather.8
  1555.0 31.8 reduce-scatter.7
  1597.9 33.1 all-gather.10
  3100.4 54.2 reduce-scatter.9
  3160.0 33.1 all-gather.12
  3194.8 33.1 all-gather.14
  3244.9 54.3 reduce-scatter.11
  3306.4 33.1 all-gather.16
  4584.3 106.7 all-reduce.5
  4693.3 30.9 reduce-scatter.13
where the time goes:
time: 4810 us; the launch traced here: 4780 us
  local copies, waits for them, and re-layouts  3160 us (66%)
  matrix products  700 us (15%)
  waiting for transfers between devices  426 us (9%)
  loops' own time  283 us (6%)
  other arithmetic  123 us (3%)
  blocking collectives  73.3 us (2%)
    while x474, local copies, waits for them, and re-layouts  976 us
    reshape x50, local copies, waits for them, and re-layouts, shift_rows(): trimmed.reshape(head_count, row_count, column_count - 1)[:, :, :key_count]  788 us
    slice x50, local copies, waits for them, and re-layouts, shift_rows(): lax.slice_in_dim(flattened, row_count - 1, row_count - 1 + row_count * (c...  466 us
    dot_general x50, local copies, waits for them, and re-layouts, block_scores(): jnp.einsum('rhe,khe->hrk', offset_part, window, preferred_element_type=jn...  437 us
    dot_general x50, matrix products, block_scores(): jnp.einsum('rhe,khe->hrk', offset_part, window, preferred_element_type=jn...  227 us
    slice x40, local copies, waits for them, and re-layouts, shift_rows(): trimmed.reshape(head_count, row_count, column_count - 1)[:, :, :key_count]  188 us
    dot_general x40, matrix products, block_scores(): jnp.einsum('rhe,che->hrc', query_part, key_part, preferred_element_type=j...  143 us
    reduce_scatter x2, waiting for transfers between devices, front(): lax.psum_scatter(head_terms, 'tensor', scatter_dimension=1, tiled=True)  109 us
  transfers between devices with their start and end apart: 12, of which 12 were waited for; matrix products, arithmetic and copies ran while one was open for 2% of the time, Pallas kernels for 0%

commit v1 on v0

v1 whole, which is shorter than its diff:
```python
import functools

import jax
import jax.numpy as jnp
from jax import lax
from jax.experimental import pallas as pl
from jax.experimental.pallas import tpu as pltpu
from jax.sharding import PartitionSpec as P

ROWS = 512
HALF = 256
epsilon = 1e-05
score_scale = 0.125
masked_score = -1e30
NN = (((1,), (0,)), ((), ()))
NT = (((1,), (1,)), ((), ()))
f32 = jnp.float32
bf16 = jnp.bfloat16


def dot(a, b, dims=NN):
    return lax.dot_general(a, b, dims, preferred_element_type=f32)


def pieces(block):
    out = [(key * ROWS, ROWS, 0) for key in range(block)]
    out.append((block * ROWS, HALF, 0))
    out.append((block * ROWS + HALF, HALF, HALF))
    return out


def chunk(index, shift, blocks):
    return pl.ds(pl.multiple_of(lax.rem(index + shift, blocks) * ROWS, ROWS), ROWS)


def forward_kernel(
    blocks, shift_ref, qo_ref, qc_ref, k_ref, v_ref, w_ref, sin_ref, cos_ref, table_ref,
    o_ref, inv_ref, e_ref, keys, values, scores, query,
):
    width = qo_ref.shape[0]
    model = table_ref.shape[1]
    half = model // 2
    block = pl.program_id(1)

    @pl.when((pl.program_id(0) == 0) & (block == 0))
    def _():
        keys[:, :model] = table_ref[...]

    @pl.when(block == 0)
    def _():
        for index in range(blocks):
            lanes = chunk(index, shift_ref[0], blocks)
            here = pl.ds(index * ROWS, ROWS)
            keys[here, model:] = k_ref[:, lanes].T
            values[:, here] = v_ref[:, lanes]

    def run(index):
        pair = dot(w_ref[...], qo_ref[...])
        up, low = pair[:half], pair[half:]
        sine, cosine = sin_ref[...], cos_ref[...]
        query[:half] = ((up * sine + low * cosine) * score_scale).astype(bf16)
        query[half:model] = ((low * sine - up * cosine) * score_scale).astype(bf16)
        query[model:] = (qc_ref[...].astype(f32) * score_scale).astype(bf16)
        top = jnp.full((8, ROWS), masked_score, f32)
        for start, count, first in pieces(index):
            part = dot(keys[start : start + count, :], query[:, first:])
            if start >= index * ROWS:
                row = lax.broadcasted_iota(jnp.int32, part.shape, 0) + (start - index * ROWS)
                col = lax.broadcasted_iota(jnp.int32, part.shape, 1) + first
                part = jnp.where(col >= row, part, masked_score)
            scores[start : start + count, first:] = part
            best = jnp.max(part.reshape(count // 8, 8, ROWS - first), axis=0)
            if first:
                best = jnp.maximum(top[:, first:], best)
                top = jnp.concatenate([top[:, :first], best], axis=1)
            else:
                top = jnp.maximum(top, best)
        peak = jnp.max(top, axis=0, keepdims=True)
        total = jnp.zeros((8, ROWS), f32)
        out = jnp.zeros((width, ROWS), f32)
        for start, count, first in pieces(index):
            weight = jnp.exp(scores[start : start + count, first:] - peak[:, first:])
            gain = jnp.sum(weight.reshape(count // 8, 8, ROWS - first), axis=0)
            rounded = weight.astype(bf16)
            e_ref[start : start + count, first:] = rounded
            add = dot(values[:, start : start + count], rounded)
            if first:
                total = jnp.concatenate([total[:, :first], total[:, first:] + gain], axis=1)
                out = jnp.concatenate([out[:, :first], out[:, first:] + add], axis=1)
            else:
                total = total + gain
                out = out + add
        inverse = 1.0 / jnp.sum(total, axis=0, keepdims=True)
        o_ref[...] = out * inverse
        inv_ref[...] = inverse

    for index in range(blocks):
        pl.when(block == index)(functools.partial(run, index))


def attend_forward(shift, qo, qc, k, v, w, sine, cosine, table):
    heads, width, seq = qo.shape
    model = table.shape[1]
    blocks = seq // ROWS
    part = pl.BlockSpec((None, width, ROWS), lambda h, i, s: (h, 0, lax.rem(i + s[0], blocks)))
    whole = pl.BlockSpec((None, width, seq), lambda h, i, s: (h, 0, 0))
    wave = pl.BlockSpec((model // 2, ROWS), lambda h, i, s: (0, i))
    return pl.pallas_call(
        functools.partial(forward_kernel, blocks),
        grid_spec=pltpu.PrefetchScalarGridSpec(
            num_scalar_prefetch=1,
            grid=(heads, blocks),
            in_specs=[
                part, part, whole, whole,
                pl.BlockSpec((None, model, width), lambda h, i, s: (h, 0, 0)),
                wave, wave,
                pl.BlockSpec((seq, model), lambda h, i, s: (0, 0), pipeline_mode=pl.Buffered(1)),
            ],
            out_specs=[
                part,
                pl.BlockSpec((None, 1, ROWS), lambda h, i, s: (h, 0, i)),
                pl.BlockSpec((None, None, seq, ROWS), lambda h, i, s: (h, i, 0, 0)),
            ],
            scratch_shapes=[
                pltpu.VMEM((seq, model + width), bf16),
                pltpu.VMEM((width, seq), bf16),
                pltpu.VMEM((seq, ROWS), f32),
                pltpu.VMEM((model + width, ROWS), bf16),
            ],
        ),
        out_shape=[
            jax.ShapeDtypeStruct((heads, width, seq), f32),
            jax.ShapeDtypeStruct((heads, 1, seq), f32),
            jax.ShapeDtypeStruct((heads, blocks, seq, ROWS), bf16),
        ],
        compiler_params=pltpu.CompilerParams(vmem_limit_bytes=56 << 20),
        cost_estimate=pl.CostEstimate(
            flops=2 * heads * seq * seq * (model + 2 * width) * 5 // 8,
            bytes_accessed=heads * seq * seq * 2,
            transcendentals=heads * seq * seq // 2,
        ),
        name="attend_forward",
    )(shift, qo, qc, k, v, w, sine, cosine, table)


def backward_kernel(
    blocks, shift_ref, e_ref, do_ref, o_ref, inv_ref, qo_ref, qc_ref, k_ref, v_ref, w_ref,
    sin_ref, cos_ref, table_ref, dq_ref, dk_ref, dv_ref, dw_ref, bias_ref,
    keys, values, small, query_acc, k_acc, v_acc, w_acc, b_acc,
):
    width = qo_ref.shape[0]
    model = table_ref.shape[0]
    half = model // 2
    block = pl.program_id(1)

    @pl.when((pl.program_id(0) == 0) & (block == 0))
    def _():
        keys[:model] = table_ref[...]

    @pl.when(block == 0)
    def _():
        for index in range(blocks):
            lanes = chunk(index, shift_ref[0], blocks)
            here = pl.ds(index * ROWS, ROWS)
            keys[model:, here] = k_ref[:, lanes]
            values[here, :] = v_ref[:, lanes].T
        k_acc[...] = jnp.zeros_like(k_acc)
        v_acc[...] = jnp.zeros_like(v_acc)
        w_acc[...] = jnp.zeros_like(w_acc)
        b_acc[...] = jnp.zeros_like(b_acc)

    def run(index):
        scaled = (do_ref[...].astype(f32) * (inv_ref[...] * score_scale)).astype(bf16)
        delta = jnp.sum(scaled.astype(f32) * o_ref[...], axis=0, keepdims=True)
        for start, count, first in pieces(index):
            weight = e_ref[start : start + count, first:]
            grad = dot(values[start : start + count, :], scaled[:, first:])
            change = (weight.astype(f32) * (grad - delta[:, first:])).astype(bf16)
            add = dot(keys[:, start : start + count], change)
            if start == 0:
                query_acc[...] = add
            else:
                query_acc[:, first:] += add
            v_acc[:, start : start + count] += dot(scaled[:, first:], weight, NT)
            k_acc[:, start : start + count] += dot(qc_ref[:, first:], change, NT)
        sine, cosine = sin_ref[...], cos_ref[...]
        up, low = query_acc[:half], query_acc[half:model]
        small[:half] = (up * sine - low * cosine).astype(bf16)
        small[half:] = (up * cosine + low * sine).astype(bf16)
        offset = dot(w_ref[...], small[...])
        content = query_acc[model:]
        dq_ref[...] = (content + offset).astype(bf16)
        w_acc[...] += dot(qo_ref[...], small[...], NT)
        for lane in range(0, ROWS, 128):
            b_acc[0] += content[:, lane : lane + 128]
            b_acc[1] += offset[:, lane : lane + 128]

    for index in range(blocks):
        pl.when(block == index)(functools.partial(run, index))

    @pl.when(block == blocks - 1)
    def _():
        for index in range(blocks):
            lanes = chunk(index, shift_ref[0], blocks)
            here = pl.ds(index * ROWS, ROWS)
            dk_ref[:, lanes] = k_acc[:, here].astype(bf16)
            dv_ref[:, lanes] = (v_acc[:, here] * (1.0 / score_scale)).astype(bf16)
        dw_ref[...] = w_acc[...]
        bias_ref[...] = b_acc[...]


def attend_backward(shift, e, do, o, inv, qo, qc, k, v, w, sine, cosine, table):
    heads, width, seq = qo.shape
    model = table.shape[0]
    blocks = seq // ROWS
    part = pl.BlockSpec((None, width, ROWS), lambda h, i, s: (h, 0, lax.rem(i + s[0], blocks)))
    whole = pl.BlockSpec((None, width, seq), lambda h, i, s: (h, 0, 0))
    wave = pl.BlockSpec((model // 2, ROWS), lambda h, i, s: (0, i))
    weight = pl.BlockSpec((None, width, model), lambda h, i, s: (h, 0, 0))
    return pl.pallas_call(
        functools.partial(backward_kernel, blocks),
        grid_spec=pltpu.PrefetchScalarGridSpec(
            num_scalar_prefetch=1,
            grid=(heads, blocks),
            in_specs=[
                pl.BlockSpec((None, None, seq, ROWS), lambda h, i, s: (h, i, 0, 0)),
                part, part,
                pl.BlockSpec((None, 1, ROWS), lambda h, i, s: (h, 0, i)),
                part, part, whole, whole, weight, wave, wave,
                pl.BlockSpec((model, seq), lambda h, i, s: (0, 0), pipeline_mode=pl.Buffered(1)),
            ],
            out_specs=[
                part, whole, whole, weight,
                pl.BlockSpec((None, 2, width, 128), lambda h, i, s: (h, 0, 0, 0)),
            ],
            scratch_shapes=[
                pltpu.VMEM((model + width, seq), bf16),
                pltpu.VMEM((seq, width), bf16),
                pltpu.VMEM((model, ROWS), bf16),
                pltpu.VMEM((model + width, ROWS), f32),
                pltpu.VMEM((width, seq), f32),
                pltpu.VMEM((width, seq), f32),
                pltpu.VMEM((width, model), f32),
                pltpu.VMEM((2, width, 128), f32),
            ],
        ),
        out_shape=[
            jax.ShapeDtypeStruct((heads, width, seq), bf16),
            jax.ShapeDtypeStruct((heads, width, seq), bf16),
            jax.ShapeDtypeStruct((heads, width, seq), bf16),
            jax.ShapeDtypeStruct((heads, width, model), f32),
            jax.ShapeDtypeStruct((heads, 2, width, 128), f32),
        ],
        compiler_params=pltpu.CompilerParams(vmem_limit_bytes=56 << 20),
        cost_estimate=pl.CostEstimate(
            flops=2 * heads * seq * seq * (model + 4 * width) * 5 // 8,
            bytes_accessed=heads * seq * seq * 2,
            transcendentals=0,
        ),
        name="attend_backward",
    )(shift, e, do, o, inv, qo, qc, k, v, w, sine, cosine, table)


def waves(seq, model):
    frequency = jnp.power(
        10000.0, -jnp.arange(0, model, 2, dtype=jnp.int32).astype(f32) / model
    )
    angle = frequency[:, None] * jnp.arange(seq, dtype=jnp.int32).astype(f32)[None, :]
    sine, cosine = jnp.sin(angle), jnp.cos(angle)
    return sine, cosine, jnp.concatenate([cosine, sine], axis=0).astype(bf16)


class Paired:
    def __init__(self, dp_count):
        self.dp_count = dp_count
        self.core = lax.rem(lax.axis_index("dp"), 2)
        self.side = lax.axis_index("tensor")
        self.index = self.core

    def trade(self, value):
        pairs = []
        for place in range(2 * self.dp_count):
            group, core, side = place // 4, place // 2 % 2, place % 2
            pairs.append((place, group * 4 + side * 2 + core))
        return lax.ppermute(value, ("dp", "tensor"), pairs)

    def cross(self, value, flip):
        return lax.ppermute(value, "dp", [(i, i ^ flip) for i in range(self.dp_count)])

    def across(self, value):
        return lax.ppermute(value, "tensor", [(0, 1), (1, 0)])

    def shift(self, blocks):
        return jnp.reshape(self.index * (blocks // 2), (1,)).astype(jnp.int32)

    def gather(self, value):
        return jnp.concatenate([value, self.cross(value, 1)], axis=0)

    def scatter(self, value):
        rows = value.shape[0] // 2
        other = self.cross(value[rows:].astype(bf16), 1)
        return value[:rows] + other.astype(f32)

    def flips(self):
        flips, flip = [], 2
        while flip < self.dp_count:
            flips.append(flip)
            flip *= 2
        return flips

    def total(self, value):
        for flip in [1] + self.flips():
            value = value + self.cross(value, flip)
        return value + self.across(value)

    def sums(self, value):
        bits = [lax.rem(lax.axis_index("dp") // flip, 2) for flip in self.flips()]
        value = value.astype(bf16)

        def halve(value, bit, move):
            rows = value.shape[0] // 2
            keep = lax.dynamic_slice_in_dim(value, bit * rows, rows, 0)
            send = lax.dynamic_slice_in_dim(value, (1 - bit) * rows, rows, 0)
            return (keep.astype(f32) + move(send).astype(f32)).astype(bf16)

        def double(value, bit, move):
            other = move(value)
            return jnp.where(
                bit == 0,
                jnp.concatenate([value, other], axis=0),
                jnp.concatenate([other, value], axis=0),
            )

        for flip, bit in zip(self.flips(), bits):
            value = halve(value, bit, functools.partial(self.cross, flip=flip))
        value = self.trade(halve(value, self.side, self.across))
        value = double(value, self.core, functools.partial(self.cross, flip=1))
        for flip, bit in reversed(list(zip(self.flips(), bits))):
            value = double(value, bit, functools.partial(self.cross, flip=flip))
        return value.astype(f32)


class Plain:
    def __init__(self, tensor_count):
        self.index = lax.axis_index("tensor")

    def trade(self, value):
        return value

    def shift(self, blocks):
        return jnp.zeros((1,), jnp.int32)

    def gather(self, value):
        return lax.all_gather(value, "tensor", axis=0, tiled=True)

    def scatter(self, value):
        return lax.psum_scatter(value, "tensor", scatter_dimension=0, tiled=True)

    def total(self, value):
        return lax.psum(value, ("dp", "tensor"))

    def sums(self, value):
        return lax.psum(value.astype(bf16), "dp").astype(f32)


def norm_rows(values, norm_gain, norm_bias):
    centre = values - jnp.mean(values, axis=-1, keepdims=True)
    inverse = lax.rsqrt(jnp.mean(centre * centre, axis=-1, keepdims=True) + epsilon)
    normal = centre * inverse
    return (normal * norm_gain + norm_bias, normal, inverse)


def norm_back(upstream, normal, inverse, norm_gain):
    scaled = upstream * norm_gain
    centred = scaled - jnp.mean(scaled, axis=-1, keepdims=True)
    centred = centred - normal * jnp.mean(scaled * normal, axis=-1, keepdims=True)
    return (
        inverse * centred,
        jnp.sum(upstream * normal, axis=0),
        jnp.sum(upstream, axis=0),
    )


def product(spec, a, b):
    return jnp.einsum(spec, a, b, preferred_element_type=f32)


def local(
    inputs, lengths, norm1_gain, norm1_bias, query_key_value_weight, content_bias, position_bias,
    pos_weight, output_weight, out_bias, norm2_gain, norm2_bias, up_projection_weight, up_bias,
    down_projection_weight, down_bias, cotangent,
):
    tensor_count = lax.axis_size("tensor")
    dp_count = lax.axis_size("dp")
    moves = Paired(dp_count) if tensor_count == 2 and dp_count % 2 == 0 else Plain(tensor_count)
    _, shard_rows, model = inputs.shape
    seq = shard_rows * tensor_count
    heads, width = content_bias.shape
    flat = heads * width
    hidden = up_bias.shape[0]
    blocks = seq // ROWS
    shift = moves.shift(blocks)
    after = lax.optimization_barrier

    row = lax.axis_index("tensor") * shard_rows + jnp.arange(shard_rows, dtype=jnp.int32)
    valid = (row < lengths[0])[:, None]

    vectors = jnp.concatenate([content_bias.reshape(-1), position_bias.reshape(-1), up_bias])
    source, qkv_weight, vectors = (
        moves.trade(inputs[0]), moves.trade(query_key_value_weight), moves.trade(vectors)
    )
    later = after((source, qkv_weight, pos_weight, output_weight, up_projection_weight))
    source, qkv_weight = later[0], later[1]
    pos_weight, out_weight = moves.trade(later[2]), moves.trade(later[3])
    up_weight = moves.trade(later[4])
    down_weight = moves.trade(after((pos_weight, down_projection_weight))[1])
    cot = jnp.where(valid, cotangent[0], jnp.zeros_like(cotangent[0]))
    cot = moves.trade(after((up_weight, cot))[1])
    content_vector, position_vector = vectors[:flat], vectors[flat : 2 * flat]
    up_vector = vectors[2 * flat :]

    sine, cosine, table_t = waves(seq, model)
    table = table_t.T

    source = source.astype(f32)
    normed1, unit1, inverse1 = norm_rows(source, norm1_gain, norm1_bias)
    first_rows = moves.gather(normed1.astype(bf16))
    projected = product("nrk,sr->nks", qkv_weight, first_rows)
    shaped = (heads, width, seq)
    query_content = (projected[0] + content_vector[:, None]).astype(bf16).reshape(shaped)
    query_offset = (projected[0] + position_vector[:, None]).astype(bf16).reshape(shaped)
    key_rows = projected[1].astype(bf16).reshape(shaped)
    value_rows = projected[2].astype(bf16).reshape(shaped)
    pos_heads = pos_weight.reshape(model, heads, width)
    attended, inverse_sum, weights = attend_forward(
        shift, query_offset, query_content, key_rows, value_rows, pos_heads.transpose(1, 0, 2),
        sine, cosine, table,
    )
    attended_low = attended.reshape(flat, seq).astype(bf16)
    branch = moves.scatter(product("ks,ku->su", attended_low, out_weight))
    middle = source + (branch + out_bias)

    normed2, unit2, inverse2 = norm_rows(middle, norm2_gain, norm2_bias)
    second_rows = moves.gather(normed2.astype(bf16))
    hidden_pre = product("sr,rk->sk", second_rows, up_weight) + up_vector
    active, gelu_pull = jax.vjp(lambda v: jax.nn.gelu(v, approximate=False), hidden_pre)
    active = active.astype(bf16)
    ffn_out = moves.scatter(product("sk,ku->su", active, down_weight)) + down_bias
    output = moves.trade((middle + ffn_out).astype(bf16))
    output = jnp.where(valid, output, jnp.zeros_like(output))

    grad_rows = cot.astype(f32)
    all_grad = moves.gather(cot)
    down_weight_grad = product("sk,su->ku", active, all_grad)
    hidden_grad = product("su,ku->sk", all_grad, down_weight)
    pre_grad = gelu_pull(hidden_grad)[0].astype(bf16)
    up_weight_grad = product("sr,sk->rk", second_rows, pre_grad)
    up_bias_grad = jnp.sum(pre_grad.astype(f32), axis=0)
    upstream2 = moves.scatter(product("sk,rk->sr", pre_grad, up_weight))
    middle_part, gain2_grad, bias2_grad = norm_back(upstream2, unit2, inverse2, norm2_gain)
    middle_grad = grad_rows + middle_part
    branch_grad = middle_grad.astype(bf16)
    all_branch = moves.gather(branch_grad)
    out_weight_grad = product("ks,su->ku", attended_low, all_branch)
    early = moves.sums(
        jnp.concatenate([up_weight_grad.reshape(-1, model), down_weight_grad, out_weight_grad])
    )
    attended_grad = product("ku,su->ks", out_weight, all_branch).astype(bf16).reshape(shaped)
    query_grad, key_grad, value_grad, pos_grad, bias_grads = attend_backward(
        shift, weights, attended_grad, attended, inverse_sum, query_offset, query_content,
        key_rows, value_rows, pos_heads.transpose(1, 2, 0), sine, cosine, table_t,
    )
    stacked = jnp.stack([query_grad, key_grad, value_grad]).reshape(3, flat, seq)
    qkv_weight_grad = product("nks,sr->nkr", stacked, first_rows)
    late = moves.sums(
        jnp.concatenate([qkv_weight_grad.reshape(3 * flat, model), pos_grad.reshape(flat, model)])
    )
    upstream1 = moves.scatter(product("nks,nrk->sr", stacked, qkv_weight))
    input_part, gain1_grad, bias1_grad = norm_back(upstream1, unit1, inverse1, norm1_gain)
    input_grad = moves.trade((middle_grad + input_part).astype(bf16)).astype(f32)

    bias_grads = jnp.sum(bias_grads, axis=-1)

    def placed(vector):
        count = vector.shape[0]
        room = jnp.zeros((count * tensor_count,), f32)
        return lax.dynamic_update_slice_in_dim(room, vector, moves.index * count, 0)

    parts = [
        gain1_grad, bias1_grad, jnp.sum(branch_grad.astype(f32), axis=0), gain2_grad, bias2_grad,
        jnp.sum(grad_rows, axis=0), placed(bias_grads[:, 0].reshape(-1)),
        placed(bias_grads[:, 1].reshape(-1)), placed(up_bias_grad),
    ]
    small = moves.total(jnp.concatenate(parts).reshape(-1, 128)).reshape(-1)
    side = lax.axis_index("tensor")
    vectors, place = [], 0
    for part in parts[:6]:
        vectors.append(small[place : place + model])
        place += model
    for count in (flat, flat, hidden):
        here = small[place : place + count * tensor_count]
        vectors.append(lax.dynamic_slice_in_dim(here, side * count, count, 0))
        place += count * tensor_count

    up_rows = model * hidden // model
    return (
        output[None],
        input_grad[None],
        vectors[0],
        vectors[1],
        late[: 3 * flat].reshape(3, flat, model).transpose(0, 2, 1),
        vectors[6].reshape(heads, width),
        vectors[7].reshape(heads, width),
        late[3 * flat :].T,
        early[up_rows + hidden :],
        vectors[2],
        vectors[3],
        vectors[4],
        early[:up_rows].reshape(model, hidden),
        vectors[8],
        early[up_rows : up_rows + hidden],
        vectors[5],
    )


def solution(mesh):
    rows = P("dp", "tensor", None)
    return jax.shard_map(
        local,
        mesh=mesh,
        in_specs=(
            rows, P("dp"), P(), P(), P(None, None, "tensor"), P("tensor", None),
            P("tensor", None), P(None, "tensor"), P("tensor", None), P(), P(), P(),
            P(None, "tensor"), P("tensor"), P("tensor", None), P(), rows,
        ),
        out_specs=(
            rows, rows, P(), P(), P(None, None, "tensor"), P("tensor", None),
            P("tensor", None), P(None, "tensor"), P("tensor", None), P(), P(), P(),
            P(None, "tensor"), P("tensor"), P("tensor", None), P(),
        ),
        check_vma=False,
    )
```

time: 4810 us -> 463 us (0.10)
  local copies, waits for them, and re-layouts: 3160 us -> 51.3 us
  matrix products: 700 us -> 67.2 us
  waiting for transfers between devices: 426 us -> 92.3 us
  loops' own time: 283 us -> 0 us
  starting transfers between devices: 0.67 us -> 96.3 us
  Pallas kernels: 0 us -> 88.2 us
  blocking collectives: 73.3 us -> 0 us
  other arithmetic: 123 us -> 58.4 us
    while x480 -> x0, local copies, waits for them, and re-layouts: 999 us -> none
    reshape x60 -> x7, local copies, waits for them, and re-layouts: 846 us -> 8.71 us  [the longest x1 3.02 us: local(): late[:3 * flat].reshape(3, flat, model).transpose(0, 2, 1)]
    slice x95 -> x14, local copies, waits for them, and re-layouts: 659 us -> 11.4 us  [the longest x4 3.79 us: scatter(): other = self.cross(value[rows:].astype(bf16), 1)]
    dot_general x196 -> x12, matrix products: 700 us -> 67.2 us  [product(): return jnp.einsum(spec, a, b, preferred_element_type=f32)]
    dot_general x54 -> x0, local copies, waits for them, and re-layouts: 442 us -> none  [the longest x50 437 us: block_scores(): jnp.einsum('rhe,khe->hrk', offset_part, window, preferred_element_type=jn...]
    another operation x23 -> x0, loops' own time: 283 us -> none  [the longest x2 105 us: attend_sequence(): lax.map(one_block, jnp.arange(block_count, dtype=jnp.int32))]
    reduce_scatter x5 -> x0, waiting for transfers between devices: 215 us -> none  [the longest x2 109 us: front(): lax.psum_scatter(head_terms, 'tensor', scatter_dimension=1, tiled=True)]
    all_gather x6 -> x0, waiting for transfers between devices: 144 us -> none  [the longest x2 65.7 us: front(): lax.all_gather(normed2.astype(jnp.bfloat16), 'tensor', axis=1, tiled=True)]
  transfers between devices with their start and end apart: 12 -> 41, of which waited for: 12 -> 12; matrix products, arithmetic and copies ran while one was open for 2% -> 26% of each run, Pallas kernels for 0% -> 9%
where the time goes in v1:
time: 463 us; the launch traced here: 456 us
  starting transfers between devices  96.3 us (21%)
  waiting for transfers between devices  92.3 us (20%)
  Pallas kernels  88.2 us (19%)
  matrix products  67.2 us (15%)
  other arithmetic  58.4 us (13%)
  local copies, waits for them, and re-layouts  51.3 us (11%)
    ppermute x26, waiting for transfers between devices, cross(): lax.ppermute(value, 'dp', [(i, i ^ flip) for i in range(self.dp_count)])  86.2 us
    dot_general x12, matrix products, product(): return jnp.einsum(spec, a, b, preferred_element_type=f32)  67.2 us
    ppermute x26, starting transfers between devices, cross(): lax.ppermute(value, 'dp', [(i, i ^ flip) for i in range(self.dp_count)])  54.8 us
    pallas_call x1, Pallas kernels, attend_backward(): pl.pallas_call(functools.partial(backward_kernel, blocks), grid_spec=pltp...  48 us
    ppermute x12, starting transfers between devices, trade(): return lax.ppermute(value, ('dp', 'tensor'), pairs)  41.3 us
    pallas_call x1, Pallas kernels, attend_forward(): pl.pallas_call(functools.partial(forward_kernel, blocks), grid_spec=pltpu...  40.2 us
    another operation x4, local copies, waits for them, and re-layouts, local(): jnp.stack([query_grad, key_grad, value_grad]).reshape(3, flat, seq)  10.1 us
    another operation x2, other arithmetic  9.89 us
  transfers between devices with their start and end apart: 41, of which 12 were waited for; matrix products, arithmetic and copies ran while one was open for 26% of the time, Pallas kernels for 9%

profile of v1, /device:TPU:0, one launch (start us, length us, event | category | flops | bytes accessed | tf_op | source)
XLA Modules:
  0.0 456.4 jit_solution(6298748935398603499)
XLA Ops:
  10.1 19.5 %collective-permute-start.2 = (bf16[1024,512]{1,0:T(8,128)(2,1)}, bf16[1024,512]{1,0:T(8,128)(2,1)}, u32[]{:S(2)}, u32[]{:S(2)}) collective-permute-start(bf16[1024,512]{1,0:T(8,128)(2,1)} %fusion.14), channel_id=1, source_target_pairs={{0,2},{2,0},{4,6},{6,4},{8,10},{10,8},{12,14},{14,12},{16,18},{18,... | collective-permute-start | bytes 3145736 | tf_op jit(solution)/shard_map/ppermute | solution.py:288
  29.7 8.8 %fusion.33 = (bf16[256,2048]{1,0:T(8,128)(2,1)S(1)}, bf16[256,2048]{1,0:T(8,128)(2,1)S(1)}, f32[256,2048]{1,0:T(8,128)}, f32[256,2048]{1,0:T(8,128)}) fusion(f32[2048]{0:T(1024)S(1)} %iota_convert_fusion, f32[256]{0:T(256)S(1)} %multiply_power_fusion), kind=kLoop, calls=%fused_computation.94 | loop fusion | flops 1572864 | bytes 6300672 | tf_op jit(solution)/shard_map/convert.12
  38.5 3.6 collective-permute-start.4
  48.2 9.6 %collective-permute-start.8 = (bf16[512,1024]{1,0:T(8,128)(2,1)}, bf16[512,1024]{1,0:T(8,128)(2,1)}, u32[]{:S(2)}, u32[]{:S(2)}) collective-permute-start(bf16[512,1024]{1,0:T(8,128)(2,1)} %param.29), channel_id=1, source_target_pairs={{0,0},{1,2},{2,1},{3,3},{4,4},{5,6},{6,5},{7,7},{8,8},{9,10},{10,9... | collective-permute-start | bytes 3145736 | tf_op jit(solution)/shard_map/ppermute | solution.py:285
  59.9 3.6 fusion.50
  66.9 40.2 %attend_forward.1 = (f32[4,64,2048]{2,1,0:T(8,128)}, f32[4,1,2048]{2,1,0:T(1,128)}, bf16[4,4,2048,512]{3,2,1,0:T(8,128)(2,1)}) custom-call(s32[1]{0:T(128)} %bitcast.2.shift_ref, bf16[4,64,2048]{2,1,0:T(8,128)(2,1)} %get-tuple-element.103.qo_ref, bf16[4,64,2048]{2,1,0:T(8,128)(2,1)} %get-tuple-element.102.qc_ref, bf16[4,64,2048]{2,1,0:T(8,128)(2,1)} %bitcast.93, ...), custom_call_target="tpu_custom_call" | custom-call | flops 13421772800 | bytes 33554432 | tf_op jit(solution)/shard_map/attend_forward/pallas_call | solution.py:108
  122.1 8.2 %collective-permute-start.13 = (bf16[1024,512]{1,0:T(8,128)(2,1)S(1)}, bf16[1024,512]{1,0:T(8,128)(2,1)S(1)}, u32[]{:S(2)}, u32[]{:S(2)}) collective-permute-start(bf16[1024,512]{1,0:T(8,128)(2,1)S(1)} %collective-permute-done.12), channel_id=1, source_target_pairs={{0,2},{2,0},{4,6},{6,4},{8,10},{10,8},{12,14},{14,12},{16,18},{18,... | collective-permute-start | bytes 3145736 | tf_op jit(solution)/shard_map/ppermute | solution.py:288
  130.3 24.5 %multiply_convert_fusion = (bf16[2048,1024]{1,0:T(8,128)(2,1)S(1)}, f32[2048,1024]{1,0:T(8,128)S(1)}, f32[2048,1024]{1,0:T(8,128)}) fusion(f32[1024]{0:T(1024)S(1)} %slice.182, bf16[512,1024]{1,0:T(8,128)(2,1)} %collective-permute-done.8, bf16[1024,512]{1,0:T(8,128)(2,1)S(1)} %collective-permute-done.7, bf16[1024,512]{1,0:T(8,128)(2,1)S(1)} %add_convert_fusion.2), kind=kOutput, calls=%fused_computation.4 | convolution fusion | flops 2290089984 | bytes 24121344 | tf_op jit(solution)/shard_map/sr,rk->sk/dot_general | solution.py:385
  155.0 10.9 %convert_reduce_fusion = (f32[1024]{0:T(1024)}, bf16[2048,1024]{1,0:T(8,128)(2,1)S(1)}) fusion(f32[2048,1024]{1,0:T(8,128)S(1)} %get-tuple-element.92, bf16[2048,512]{1,0:T(8,128)(2,1)S(1)} %constant_dynamic-update-slice_fusion, bf16[1024,512]{1,0:T(8,128)(2,1)S(1)} %collective-permute-done.9, f32[2048,1024]{1,0:T(8,128)} %get-tuple-element.121, ...), kind=kOutput, calls=%fused_computation.2 | convolution fusion | flops 2183134208 | bytes 24125440 | tf_op jit(solution)/shard_map/su,ku->sk/dot_general | solution.py:385
  165.9 4.4 fusion.53
  176.7 3.9 multiply_reduce_fusion
  180.7 5.2 %convert_reduce_fusion.3 = (f32[512]{0:T(512)}, bf16[1024,512]{1,0:T(8,128)(2,1)}, f32[1024,512]{1,0:T(8,128)}, bf16[1024,512]{1,0:T(8,128)(2,1)}, f32[512]{0:T(512)}) fusion(f32[1024]{0:T(1024)S(1)} %get-tuple-element.124, f32[1024,512]{1,0:T(8,128)S(1)} %get-tuple-element.94, f32[1024]{0:T(1024)S(1)} %broadcast_multiply_fusion.4, ...), kind=kLoop, calls=%fused_computation.66 | loop fusion | flops 10484736 | bytes 13656064 | tf_op jit(solution)/shard_map/reduce_sum | solution.py:490
  189.7 6.2 %convolution_convert_fusion.1 = bf16[1024,512]{1,0:T(8,128)(2,1)} fusion(bf16[2048,1024]{1,0:T(8,128)(2,1)} %copy-done.47, bf16[2048,512]{1,0:T(8,128)(2,1)} %copy-done.21), kind=kOutput, calls=%fused_computation.75 | convolution fusion | flops 2148007936 | bytes 7340032 | tf_op jit(solution)/shard_map/sk,su->ku/dot_general | solution.py:385
  196.0 3.3 convolution_convert_fusion
  199.3 48.0 %attend_backward.1 = (bf16[4,64,2048]{2,1,0:T(8,128)(2,1)}, bf16[4,64,2048]{2,1,0:T(8,128)(2,1)}, bf16[4,64,2048]{2,1,0:T(8,128)(2,1)}, f32[4,64,512]{2,1,0:T(8,128)}, f32[4,2,64,128]{3,2,1,0:T(8,128)}) custom-call(s32[1]{0:T(128)} %bitcast.2.shift_ref, bf16[4,4,2048,512]{3,2,1,0:T(8,128)(2,1)} %get-tuple-element.39.e_ref, bf16[4,64,2048]{2,1,0:T(8,128)(2,1)} %bitcast.97, ...), custom_call_target="tpu_custom_call" | custom-call | flops 16106127360 | bytes 33554432 | tf_op jit(solution)/shard_map/attend_backward/pallas_call | solution.py:220
  252.6 3.2 pad_maximum_fusion
  255.8 4.9 %copy.49 = bf16[3,256,2048]{2,1,0:T(8,128)(2,1)} copy(bf16[3,256,2048]{1,2,0:T(8,128)(2,1)} %pad_maximum_fusion) | data formatting | bytes 6291456 | tf_op jit(solution)/shard_map/stack | solution.py:473
  261.9 4.4 convolution_convert_fusion.3
  274.1 7.0 %collective-permute-done.23 = bf16[512,512]{1,0:T(8,128)(2,1)S(1)} collective-permute-done((bf16[512,512]{1,0:T(8,128)(2,1)S(1)}, bf16[512,512]{1,0:T(8,128)(2,1)S(1)}, u32[]{:S(2)}, u32[]{:S(2)}) %collective-permute-start.23) | collective-permute-done | bytes 524320 | tf_op jit(solution)/shard_map/ppermute | solution.py:288
  283.6 5.9 %collective-permute-done.24 = bf16[256,512]{1,0:T(8,128)(2,1)S(1)} collective-permute-done((bf16[256,512]{1,0:T(8,128)(2,1)S(1)}, bf16[256,512]{1,0:T(8,128)(2,1)S(1)}, u32[]{:S(2)}, u32[]{:S(2)}) %collective-permute-start.24) | collective-permute-done | bytes 262176 | tf_op jit(solution)/shard_map/ppermute | solution.py:288
  296.4 9.4 %collective-permute-start.11 = (bf16[1024,512]{1,0:T(8,128)(2,1)}, bf16[1024,512]{1,0:T(8,128)(2,1)}, u32[]{:S(2)}, u32[]{:S(2)}) collective-permute-start(bf16[1024,512]{1,0:T(8,128)(2,1)} %get-tuple-element.101), channel_id=1, source_target_pairs={{0,0},{1,2},{2,1},{3,3},{4,4},{5,6},{6,5},{7,7},{8,8},{9,10},{10,9... | collective-permute-start | bytes 3145736 | tf_op jit(solution)/shard_map/ppermute | solution.py:285
  318.7 3.2 fusion.20
  325.4 12.0 %collective-permute-done.33 = bf16[576,512]{1,0:T(8,128)(2,1)S(1)} collective-permute-done((bf16[576,512]{1,0:T(8,128)(2,1)S(1)}, bf16[576,512]{1,0:T(8,128)(2,1)S(1)}, u32[]{:S(2)}, u32[]{:S(2)}) %collective-permute-start.33) | collective-permute-done | bytes 589856 | tf_op jit(solution)/shard_map/ppermute | solution.py:288
  340.2 13.5 %collective-permute-done.34 = bf16[288,512]{1,0:T(8,128)(2,1)S(1)} collective-permute-done((bf16[288,512]{1,0:T(8,128)(2,1)S(1)}, bf16[288,512]{1,0:T(8,128)(2,1)S(1)}, u32[]{:S(2)}, u32[]{:S(2)}) %collective-permute-start.34) | collective-permute-done | bytes 294944 | tf_op jit(solution)/shard_map/ppermute | solution.py:288
  354.5 6.1 %collective-permute-done.35 = bf16[144,512]{1,0:T(8,128)(2,1)S(1)} collective-permute-done((bf16[144,512]{1,0:T(8,128)(2,1)S(1)}, bf16[144,512]{1,0:T(8,128)(2,1)S(1)}, u32[]{:S(2)}, u32[]{:S(2)}) %collective-permute-start.35) | collective-permute-done | bytes 147488 | tf_op jit(solution)/shard_map/ppermute | solution.py:291
  362.7 4.4 collective-permute-start.37
  371.7 16.4 %collective-permute-done.38 = bf16[288,512]{1,0:T(8,128)(2,1)S(1)} collective-permute-done((bf16[288,512]{1,0:T(8,128)(2,1)S(1)}, bf16[288,512]{1,0:T(8,128)(2,1)S(1)}, u32[]{:S(2)}, u32[]{:S(2)}) %collective-permute-start.38) | collective-permute-done | bytes 294944 | tf_op jit(solution)/shard_map/ppermute | solution.py:288
  394.0 9.8 %collective-permute-start.17 = (bf16[1024,512]{1,0:T(8,128)(2,1)}, bf16[1024,512]{1,0:T(8,128)(2,1)}, u32[]{:S(2)}, u32[]{:S(2)}) collective-permute-start(bf16[1024,512]{1,0:T(8,128)(2,1)} %fusion.19), channel_id=1, source_target_pairs={{0,0},{1,2},{2,1},{3,3},{4,4},{5,6},{6,5},{7,7},{8,8},{9,10},{10,9... | collective-permute-start | bytes 3145736 | tf_op jit(solution)/shard_map/ppermute | solution.py:285
  403.9 5.7 %collective-permute-done.30 = bf16[256,512]{1,0:T(8,128)(2,1)S(1)} collective-permute-done((bf16[256,512]{1,0:T(8,128)(2,1)S(1)}, bf16[256,512]{1,0:T(8,128)(2,1)S(1)}, u32[]{:S(2)}, u32[]{:S(2)}) %collective-permute-start.30) | collective-permute-done | bytes 262176 | tf_op jit(solution)/shard_map/ppermute | solution.py:288
  418.6 6.2 %collective-permute-done.31 = bf16[512,512]{1,0:T(8,128)(2,1)S(1)} collective-permute-done((bf16[512,512]{1,0:T(8,128)(2,1)S(1)}, bf16[512,512]{1,0:T(8,128)(2,1)S(1)}, u32[]{:S(2)}, u32[]{:S(2)}) %collective-permute-start.31) | collective-permute-done | bytes 524320 | tf_op jit(solution)/shard_map/ppermute | solution.py:288
  433.3 15.4 %collective-permute-done.40 = bf16[1152,512]{1,0:T(8,128)(2,1)} collective-permute-done((bf16[1152,512]{1,0:T(8,128)(2,1)}, bf16[1152,512]{1,0:T(8,128)(2,1)}, u32[]{:S(2)}, u32[]{:S(2)}) %collective-permute-start.40) | collective-permute-done | bytes 1179680 | tf_op jit(solution)/shard_map/ppermute | solution.py:288
  448.7 3.2 fusion.12
  (280 shorter events, 122.8 us)
Async XLA Ops:
  6.5 39.9 %collective-permute-start.3 = (f32[1536]{0:T(1024)S(1)}, f32[1536]{0:T(1024)S(1)}, u32[]{:S(2)}, u32[]{:S(2)}) collective-permute-start(f32[1536]{0:T(1024)S(1)} %pad_maximum_fusion.14), channel_id=1, source_target_pairs={{0,0},{1,2},{2,1},{3,3},{4,4},{5,6},{6,5},{7,7},{8,8},{9,10},{10,9... | collective-permute-start | bytes 18440 | tf_op jit(solution)/shard_map/ppermute | solution.py:285
  10.1 49.8 %collective-permute-start.2 = (bf16[1024,512]{1,0:T(8,128)(2,1)}, bf16[1024,512]{1,0:T(8,128)(2,1)}, u32[]{:S(2)}, u32[]{:S(2)}) collective-permute-start(bf16[1024,512]{1,0:T(8,128)(2,1)} %fusion.14), channel_id=1, source_target_pairs={{0,2},{2,0},{4,6},{6,4},{8,10},{10,8},{12,14},{14,12},{16,18},{18,... | collective-permute-start | bytes 3145736 | tf_op jit(solution)/shard_map/ppermute | solution.py:288
  38.5 19.3 %collective-permute-start.4 = (bf16[512,256]{1,0:T(8,128)(2,1)}, bf16[512,256]{1,0:T(8,128)(2,1)}, u32[]{:S(2)}, u32[]{:S(2)}) collective-permute-start(bf16[512,256]{1,0:T(8,128)(2,1)} %param.24), channel_id=1, source_target_pairs={{0,0},{1,2},{2,1},{3,3},{4,4},{5,6},{6,5},{7,7},{8,8},{9,10},{10,9... | collective-permute-start | bytes 786440 | tf_op jit(solution)/shard_map/ppermute | solution.py:285
  46.6 62.2 %collective-permute-start.5 = (bf16[256,512]{1,0:T(8,128)(2,1)}, bf16[256,512]{1,0:T(8,128)(2,1)S(1)}, u32[]{:S(2)}, u32[]{:S(2)}) collective-permute-start(bf16[256,512]{1,0:T(8,128)(2,1)} %param.25), channel_id=1, source_target_pairs={{0,0},{1,2},{2,1},{3,3},{4,4},{5,6},{6,5},{7,7},{8,8},{9,10},{10,9... | collective-permute-start | bytes 786440 | tf_op jit(solution)/shard_map/ppermute | solution.py:285
  48.2 65.7 %collective-permute-start.8 = (bf16[512,1024]{1,0:T(8,128)(2,1)}, bf16[512,1024]{1,0:T(8,128)(2,1)}, u32[]{:S(2)}, u32[]{:S(2)}) collective-permute-start(bf16[512,1024]{1,0:T(8,128)(2,1)} %param.29), channel_id=1, source_target_pairs={{0,0},{1,2},{2,1},{3,3},{4,4},{5,6},{6,5},{7,7},{8,8},{9,10},{10,9... | collective-permute-start | bytes 3145736 | tf_op jit(solution)/shard_map/ppermute | solution.py:285
  113.9 8.1 %collective-permute-start.12 = (bf16[1024,512]{1,0:T(8,128)(2,1)S(1)}, bf16[1024,512]{1,0:T(8,128)(2,1)S(1)}, u32[]{:S(2)}, u32[]{:S(2)}) collective-permute-start(bf16[1024,512]{1,0:T(8,128)(2,1)S(1)} %bitcast_select_fusion), channel_id=1, source_target_pairs={{0,0},{1,2},{2,1},{3,3},{4,4},{5,6},{6,5},{7,7},{8,8},{9,10},{10,9... | collective-permute-start | bytes 3145736 | tf_op jit(solution)/shard_map/ppermute | solution.py:285
  118.7 11.6 %collective-permute-start.7 = (bf16[1024,512]{1,0:T(8,128)(2,1)S(1)}, bf16[1024,512]{1,0:T(8,128)(2,1)S(1)}, u32[]{:S(2)}, u32[]{:S(2)}) collective-permute-start(bf16[1024,512]{1,0:T(8,128)(2,1)S(1)} %add_convert_fusion.2), channel_id=1, source_target_pairs={{0,2},{2,0},{4,6},{6,4},{8,10},{10,8},{12,14},{14,12},{16,18},{18,... | collective-permute-start | bytes 3145736 | tf_op jit(solution)/shard_map/ppermute | solution.py:288
  121.3 33.6 %collective-permute-start.9 = (bf16[1024,512]{1,0:T(8,128)(2,1)S(1)}, bf16[1024,512]{1,0:T(8,128)(2,1)S(1)}, u32[]{:S(2)}, u32[]{:S(2)}) collective-permute-start(bf16[1024,512]{1,0:T(8,128)(2,1)S(1)} %copy-done.42), channel_id=1, source_target_pairs={{0,0},{1,2},{2,1},{3,3},{4,4},{5,6},{6,5},{7,7},{8,8},{9,10},{10,9... | collective-permute-start | bytes 3145736 | tf_op jit(solution)/shard_map/ppermute | solution.py:285
  122.1 32.8 %collective-permute-start.13 = (bf16[1024,512]{1,0:T(8,128)(2,1)S(1)}, bf16[1024,512]{1,0:T(8,128)(2,1)S(1)}, u32[]{:S(2)}, u32[]{:S(2)}) collective-permute-start(bf16[1024,512]{1,0:T(8,128)(2,1)S(1)} %collective-permute-done.12), channel_id=1, source_target_pairs={{0,2},{2,0},{4,6},{6,4},{8,10},{10,8},{12,14},{14,12},{16,18},{18,... | collective-permute-start | bytes 3145736 | tf_op jit(solution)/shard_map/ppermute | solution.py:288
  185.9 10.1 %collective-permute-start.15 = (bf16[1024,512]{1,0:T(8,128)(2,1)}, bf16[1024,512]{1,0:T(8,128)(2,1)S(1)}, u32[]{:S(2)}, u32[]{:S(2)}) collective-permute-start(bf16[1024,512]{1,0:T(8,128)(2,1)} %get-tuple-element.89), channel_id=1, source_target_pairs={{0,2},{2,0},{4,6},{6,4},{8,10},{10,8},{12,14},{14,12},{16,18},{18,... | collective-permute-start | bytes 3145736 | tf_op jit(solution)/shard_map/ppermute | solution.py:288
  266.9 14.2 %collective-permute-start.23 = (bf16[512,512]{1,0:T(8,128)(2,1)S(1)}, bf16[512,512]{1,0:T(8,128)(2,1)S(1)}, u32[]{:S(2)}, u32[]{:S(2)}) collective-permute-start(bf16[512,512]{1,0:T(8,128)(2,1)S(1)} %fusion.34), channel_id=1, source_target_pairs={{0,4},{2,6},{4,0},{6,2},{8,12},{10,14},{12,8},{14,10},{16,20},{18,... | collective-permute-start | bytes 1572872 | tf_op jit(solution)/shard_map/ppermute | solution.py:288
  271.6 47.1 %collective-permute-start.16 = (bf16[1024,512]{1,0:T(8,128)(2,1)}, bf16[1024,512]{1,0:T(8,128)(2,1)}, u32[]{:S(2)}, u32[]{:S(2)}) collective-permute-start(bf16[1024,512]{1,0:T(8,128)(2,1)} %slice.255), channel_id=1, source_target_pairs={{0,2},{2,0},{4,6},{6,4},{8,10},{10,8},{12,14},{14,12},{16,18},{18,... | collective-permute-start | bytes 3145736 | tf_op jit(solution)/shard_map/ppermute | solution.py:288
  281.8 7.7 %collective-permute-start.24 = (bf16[256,512]{1,0:T(8,128)(2,1)S(1)}, bf16[256,512]{1,0:T(8,128)(2,1)S(1)}, u32[]{:S(2)}, u32[]{:S(2)}) collective-permute-start(bf16[256,512]{1,0:T(8,128)(2,1)S(1)} %constant_dynamic-slice_fusion.6), channel_id=1, source_target_pairs={{0,8},{2,10},{4,12},{6,14},{8,0},{10,2},{12,4},{14,6},{16,24},{18,... | collective-permute-start | bytes 786440 | tf_op jit(solution)/shard_map/ppermute | solution.py:288
  290.3 17.2 %collective-permute-start.25 = (bf16[128,512]{1,0:T(8,128)(2,1)S(1)}, bf16[128,512]{1,0:T(8,128)(2,1)}, u32[]{:S(2)}, u32[]{:S(2)}) collective-permute-start(bf16[128,512]{1,0:T(8,128)(2,1)S(1)} %constant_dynamic-slice_fusion.5), channel_id=1, source_target_pairs={{0,16},{2,18},{4,20},{6,22},{8,24},{10,26},{12,28},{14,30},{16,0},... | collective-permute-start | bytes 393224 | tf_op jit(solution)/shard_map/ppermute | solution.py:288
  294.1 27.8 %collective-permute-start.32 = (bf16[1152,512]{1,0:T(8,128)(2,1)}, bf16[1152,512]{1,0:T(8,128)(2,1)}, u32[]{:S(2)}, u32[]{:S(2)}) collective-permute-start(bf16[1152,512]{1,0:T(8,128)(2,1)} %constant_dynamic-slice_fusion.3), channel_id=1, source_target_pairs={{0,4},{2,6},{4,0},{6,2},{8,12},{10,14},{12,8},{14,10},{16,20},{18,... | collective-permute-start | bytes 3538952 | tf_op jit(solution)/shard_map/ppermute | solution.py:288
  296.4 117.1 %collective-permute-start.11 = (bf16[1024,512]{1,0:T(8,128)(2,1)}, bf16[1024,512]{1,0:T(8,128)(2,1)}, u32[]{:S(2)}, u32[]{:S(2)}) collective-permute-start(bf16[1024,512]{1,0:T(8,128)(2,1)} %get-tuple-element.101), channel_id=1, source_target_pairs={{0,0},{1,2},{2,1},{3,3},{4,4},{5,6},{6,5},{7,7},{8,8},{9,10},{10,9... | collective-permute-start | bytes 3145736 | tf_op jit(solution)/shard_map/ppermute | solution.py:285
  309.2 7.9 %collective-permute-start.26 = (bf16[64,512]{1,0:T(8,128)(2,1)}, bf16[64,512]{1,0:T(8,128)(2,1)}, u32[]{:S(2)}, u32[]{:S(2)}) collective-permute-start(bf16[64,512]{1,0:T(8,128)(2,1)} %constant_dynamic-slice_fusion.4), channel_id=1, source_target_pairs={{0,1},{1,0},{2,3},{3,2},{4,5},{5,4},{6,7},{7,6},{8,9},{9,8},{10,11... | collective-permute-start | bytes 196616 | tf_op jit(solution)/shard_map/ppermute | solution.py:291
  317.9 43.3 %collective-permute-start.27 = (bf16[64,512]{1,0:T(8,128)(2,1)S(1)}, bf16[64,512]{1,0:T(8,128)(2,1)S(1)}, u32[]{:S(2)}, u32[]{:S(2)}) collective-permute-start(bf16[64,512]{1,0:T(8,128)(2,1)S(1)} %add_convert_fusion.11), channel_id=1, source_target_pairs={{0,0},{1,2},{2,1},{3,3},{4,4},{5,6},{6,5},{7,7},{8,8},{9,10},{10,9... | collective-permute-start | bytes 196616 | tf_op jit(solution)/shard_map/ppermute | solution.py:285
  323.6 13.8 %collective-permute-start.33 = (bf16[576,512]{1,0:T(8,128)(2,1)S(1)}, bf16[576,512]{1,0:T(8,128)(2,1)S(1)}, u32[]{:S(2)}, u32[]{:S(2)}) collective-permute-start(bf16[576,512]{1,0:T(8,128)(2,1)S(1)} %constant_dynamic-slice_fusion.2), channel_id=1, source_target_pairs={{0,8},{2,10},{4,12},{6,14},{8,0},{10,2},{12,4},{14,6},{16,24},{18,... | collective-permute-start | bytes 1769480 | tf_op jit(solution)/shard_map/ppermute | solution.py:288
  337.6 16.0 %collective-permute-start.34 = (bf16[288,512]{1,0:T(8,128)(2,1)S(1)}, bf16[288,512]{1,0:T(8,128)(2,1)S(1)}, u32[]{:S(2)}, u32[]{:S(2)}) collective-permute-start(bf16[288,512]{1,0:T(8,128)(2,1)S(1)} %constant_dynamic-slice_fusion.1), channel_id=1, source_target_pairs={{0,16},{2,18},{4,20},{6,22},{8,24},{10,26},{12,28},{14,30},{16,0},... | collective-permute-start | bytes 884744 | tf_op jit(solution)/shard_map/ppermute | solution.py:288
  338.1 15.8 %collective-permute-start.18 = (f32[48,128]{1,0:T(8,128)S(1)}, f32[48,128]{1,0:T(8,128)S(1)}, u32[]{:S(2)}, u32[]{:S(2)}) collective-permute-start(f32[48,128]{1,0:T(8,128)S(1)} %bitcast.95), channel_id=1, source_target_pairs={{0,2},{2,0},{4,6},{6,4},{8,10},{10,8},{12,14},{14,12},{16,18},{18,... | collective-permute-start | bytes 73736 | tf_op jit(solution)/shard_map/ppermute | solution.py:288
  353.9 13.3 %collective-permute-start.19 = (f32[48,128]{1,0:T(8,128)S(1)}, f32[48,128]{1,0:T(8,128)S(1)}, u32[]{:S(2)}, u32[]{:S(2)}) collective-permute-start(f32[48,128]{1,0:T(8,128)S(1)} %bitcast_add_fusion), channel_id=1, source_target_pairs={{0,4},{2,6},{4,0},{6,2},{8,12},{10,14},{12,8},{14,10},{16,20},{18,... | collective-permute-start | bytes 73736 | tf_op jit(solution)/shard_map/ppermute | solution.py:288
  361.3 7.3 %collective-permute-start.28 = (bf16[64,512]{1,0:T(8,128)(2,1)S(1)}, bf16[64,512]{1,0:T(8,128)(2,1)S(1)}, u32[]{:S(2)}, u32[]{:S(2)}) collective-permute-start(bf16[64,512]{1,0:T(8,128)(2,1)S(1)} %collective-permute-done.27), channel_id=1, source_target_pairs={{0,2},{2,0},{4,6},{6,4},{8,10},{10,8},{12,14},{14,12},{16,18},{18,... | collective-permute-start | bytes 196616 | tf_op jit(solution)/shard_map/ppermute | solution.py:288
  368.2 19.8 %collective-permute-start.38 = (bf16[288,512]{1,0:T(8,128)(2,1)S(1)}, bf16[288,512]{1,0:T(8,128)(2,1)S(1)}, u32[]{:S(2)}, u32[]{:S(2)}) collective-permute-start(bf16[288,512]{1,0:T(8,128)(2,1)S(1)} %maximum_select_fusion.5), channel_id=1, source_target_pairs={{0,16},{2,18},{4,20},{6,22},{8,24},{10,26},{12,28},{14,30},{16,0},... | collective-permute-start | bytes 884744 | tf_op jit(solution)/shard_map/ppermute | solution.py:288
  368.6 22.3 %collective-permute-start.29 = (bf16[128,512]{1,0:T(8,128)(2,1)S(1)}, bf16[128,512]{1,0:T(8,128)(2,1)S(1)}, u32[]{:S(2)}, u32[]{:S(2)}) collective-permute-start(bf16[128,512]{1,0:T(8,128)(2,1)S(1)} %maximum_select_fusion.7), channel_id=1, source_target_pairs={{0,16},{2,18},{4,20},{6,22},{8,24},{10,26},{12,28},{14,30},{16,0},... | collective-permute-start | bytes 393224 | tf_op jit(solution)/shard_map/ppermute | solution.py:288
  371.4 32.4 %collective-permute-start.21 = (f32[48,128]{1,0:T(8,128)S(1)}, f32[48,128]{1,0:T(8,128)S(1)}, u32[]{:S(2)}, u32[]{:S(2)}) collective-permute-start(f32[48,128]{1,0:T(8,128)S(1)} %add.248), channel_id=1, source_target_pairs={{0,16},{2,18},{4,20},{6,22},{8,24},{10,26},{12,28},{14,30},{16,0},... | collective-permute-start | bytes 73736 | tf_op jit(solution)/shard_map/ppermute | solution.py:288
  388.3 22.1 %collective-permute-start.39 = (bf16[576,512]{1,0:T(8,128)(2,1)S(1)}, bf16[576,512]{1,0:T(8,128)(2,1)S(1)}, u32[]{:S(2)}, u32[]{:S(2)}) collective-permute-start(bf16[576,512]{1,0:T(8,128)(2,1)S(1)} %maximum_select_fusion.3), channel_id=1, source_target_pairs={{0,8},{2,10},{4,12},{6,14},{8,0},{10,2},{12,4},{14,6},{16,24},{18,... | collective-permute-start | bytes 1769480 | tf_op jit(solution)/shard_map/ppermute | solution.py:288
  391.0 18.7 %collective-permute-start.30 = (bf16[256,512]{1,0:T(8,128)(2,1)S(1)}, bf16[256,512]{1,0:T(8,128)(2,1)S(1)}, u32[]{:S(2)}, u32[]{:S(2)}) collective-permute-start(bf16[256,512]{1,0:T(8,128)(2,1)S(1)} %maximum_select_fusion.6), channel_id=1, source_target_pairs={{0,8},{2,10},{4,12},{6,14},{8,0},{10,2},{12,4},{14,6},{16,24},{18,... | collective-permute-start | bytes 786440 | tf_op jit(solution)/shard_map/ppermute | solution.py:288
  394.0 36.4 %collective-permute-start.17 = (bf16[1024,512]{1,0:T(8,128)(2,1)}, bf16[1024,512]{1,0:T(8,128)(2,1)}, u32[]{:S(2)}, u32[]{:S(2)}) collective-permute-start(bf16[1024,512]{1,0:T(8,128)(2,1)} %fusion.19), channel_id=1, source_target_pairs={{0,0},{1,2},{2,1},{3,3},{4,4},{5,6},{6,5},{7,7},{8,8},{9,10},{10,9... | collective-permute-start | bytes 3145736 | tf_op jit(solution)/shard_map/ppermute | solution.py:285
  403.8 12.1 %collective-permute-start.22 = (f32[48,128]{1,0:T(8,128)S(1)}, f32[48,128]{1,0:T(8,128)S(1)}, u32[]{:S(2)}, u32[]{:S(2)}) collective-permute-start(f32[48,128]{1,0:T(8,128)S(1)} %add.249), channel_id=1, source_target_pairs={{0,1},{1,0},{2,3},{3,2},{4,5},{5,4},{6,7},{7,6},{8,9},{9,8},{10,11... | collective-permute-start | bytes 73736 | tf_op jit(solution)/shard_map/ppermute | solution.py:291
  409.8 14.9 %collective-permute-start.31 = (bf16[512,512]{1,0:T(8,128)(2,1)S(1)}, bf16[512,512]{1,0:T(8,128)(2,1)S(1)}, u32[]{:S(2)}, u32[]{:S(2)}) collective-permute-start(bf16[512,512]{1,0:T(8,128)(2,1)S(1)} %maximum_select_fusion.4), channel_id=1, source_target_pairs={{0,4},{2,6},{4,0},{6,2},{8,12},{10,14},{12,8},{14,10},{16,20},{18,... | collective-permute-start | bytes 1572872 | tf_op jit(solution)/shard_map/ppermute | solution.py:288
  412.0 36.7 %collective-permute-start.40 = (bf16[1152,512]{1,0:T(8,128)(2,1)}, bf16[1152,512]{1,0:T(8,128)(2,1)}, u32[]{:S(2)}, u32[]{:S(2)}) collective-permute-start(bf16[1152,512]{1,0:T(8,128)(2,1)} %maximum_select_fusion.1), channel_id=1, source_target_pairs={{0,4},{2,6},{4,0},{6,2},{8,12},{10,14},{12,8},{14,10},{16,20},{18,... | collective-permute-start | bytes 3538952 | tf_op jit(solution)/shard_map/ppermute | solution.py:288
  (59 other events, 673.2 us)
